TPU v7x, 32 devices: a whole 2x2x4 slice. The times are simulated.
32 devices in a mesh: hst: 4 (over x, core), dev: 8 (over z, y).
Axes of the slice: x: 2, y: 2, z: 4, core: 2. Of those that a mesh axis runs over, the one named last changes fastest.
Arguments:
- features: float32 [524288, 128], P(('hst', 'dev')), may hold values from -6 to 6
- requests: int32 [1024, 256], P(('hst', 'dev')), may hold values from 0 to 16383
- adjacent_one: int32 [135168, 15], P(('hst', 'dev')), may hold values from 0 to 8191, as said below
- adjacent_two: int32 [12288, 10], P(('hst', 'dev')), may hold values from 0 to 4223
- adjacent_three: int32 [2048, 5], P(('hst', 'dev')), may hold values from 0 to 383
- valid_one: int32 [135168, 15], P(('hst', 'dev')), may hold values from 0 to 1, as said below
- valid_two: int32 [12288, 10], P(('hst', 'dev')), may hold values from 0 to 1
- valid_three: int32 [2048, 5], P(('hst', 'dev')), may hold values from 0 to 1
- labels: int32 [2048], P(('hst', 'dev')), may hold values from 0 to 171
- labelled: int32 [2048], P(('hst', 'dev')), may hold values from 0 to 1, as said below
- weights_in: float32 [2, 128, 256], replicated, may hold values from -0.5 to 0.5
- weights_mid: float32 [2, 256, 256], replicated, may hold values from -0.375 to 0.375
- weights_out: float32 [2, 256, 172], replicated, may hold values from -0.375 to 0.375
- biases: float32 [684], replicated, may hold values from -0.6 to 0.6
- moment_one: float32 [684], replicated, may hold values from -0.0007954951 to 0.0007954951
- moment_two: float32 [684], replicated, may hold values from 6.1035155e-07 to 2.4414062e-06
- step_count: int32 [], replicated, may hold values from 2 to 20
- left_in: float32 [2, 128, 128], replicated, as said below
- left_mid: float32 [2, 256, 256], replicated, as said below
- left_out: float32 [2, 256, 256], replicated, as said below
- right_in: float32 [2, 256, 256], replicated, as said below
- right_mid: float32 [2, 256, 256], replicated, as said below
- right_out: float32 [2, 172, 172], replicated, as said below
- invleft_in: float32 [2, 128, 128], replicated, as said below
- invleft_mid: float32 [2, 256, 256], replicated, as said below
- invleft_out: float32 [2, 256, 256], replicated, as said below
- invright_in: float32 [2, 256, 256], replicated, as said below
- invright_mid: float32 [2, 256, 256], replicated, as said below
- invright_out: float32 [2, 172, 172], replicated, as said below
Outputs:
- loss: float32 [], replicated
- new_weights_in: float32 [2, 128, 256], replicated
- new_weights_mid: float32 [2, 256, 256], replicated
- new_weights_out: float32 [2, 256, 172], replicated
- copy_in: bfloat16 [2, 128, 256], replicated
- copy_mid: bfloat16 [2, 256, 256], replicated
- copy_out: bfloat16 [2, 256, 172], replicated
- new_left_in: float32 [2, 128, 128], replicated
- new_left_mid: float32 [2, 256, 256], replicated
- new_left_out: float32 [2, 256, 256], replicated
- new_right_in: float32 [2, 256, 256], replicated
- new_right_mid: float32 [2, 256, 256], replicated
- new_right_out: float32 [2, 172, 172], replicated
- new_biases: float32 [684], replicated
- new_moment_one: float32 [684], replicated
- new_moment_two: float32 [684], replicated
Inputs may be any that keep to these rules, and one draw needn't show every extreme that they name: `adjacent_one`: every one of a device's 8192 pulled slots is named by some entry of its rows. `valid_one`: valid shares differ from device to device. The first seed of every device is labelled. `left_in`: a positive multiple of the identity in each of the two matrices. `left_mid`: a positive multiple of the identity in each of the two matrices. `left_out`: a positive multiple of the identity in each of the two matrices. `right_in`: a positive multiple of the identity in each of the two matrices. `right_mid`: a positive multiple of the identity in each of the two matrices. `right_out`: a positive multiple of the identity in each of the two matrices. `invleft_in`: symmetric. `invleft_mid`: symmetric. `invleft_out`: symmetric. `invright_in`: symmetric. `invright_mid`: symmetric. `invright_out`: symmetric.
All inputs are finite; a program needn't handle non-finite values.
Results may differ from a plain program's by a relative error of at most 0.0094.
Values may be sent and summed in bfloat16 or wider, within the bound.
No kernel may reach another device: no remote copies, remote signals or barrier semaphores. Data moves between devices by JAX's collectives and lax.ppermute only.
A program may use at most 128 MiB of HBM per device.

v0:
```python
import jax
import jax.numpy as jnp
from jax import lax
from jax.sharding import PartitionSpec as P

highest = lax.Precision.HIGHEST


def pull_features(features, requests):
    width = features.shape[1]
    found = features[
        lax.all_to_all(requests, ("hst", "dev"), split_axis=0, concat_axis=0, tiled=True)
    ].astype(jnp.bfloat16)
    arrived = lax.all_to_all(found, ("hst", "dev"), split_axis=0, concat_axis=0, tiled=True)
    return arrived.reshape(-1, width)


def mask_counts(valid_mask):
    weights = valid_mask.astype(jnp.float32)
    return (weights, jnp.maximum(jnp.sum(weights, axis=1), 1.0))


def forward_layer(source, adjacent, valid_mask, weight, bias_row):
    weights, counts = mask_counts(valid_mask)
    summed = jnp.zeros((adjacent.shape[0], source.shape[1]), jnp.float32)
    for column in range(adjacent.shape[1]):
        summed = (
            summed
            + source[adjacent[:, column]].astype(jnp.float32) * weights[:, column : column + 1]
        )
    mixed = (summed / counts[:, None]).astype(jnp.bfloat16)
    selfrows = source[: adjacent.shape[0]]
    preact = (
        jnp.dot(selfrows, weight[0], preferred_element_type=jnp.float32)
        + jnp.dot(mixed, weight[1], preferred_element_type=jnp.float32)
        + bias_row
    )
    return (preact, mixed)


def silu_slope(preact):
    sigma = jax.nn.sigmoid(preact)
    return sigma * (1.0 + preact * (1.0 - sigma))


def contract_rows(left_side, right_side):
    return lax.dot_general(
        left_side, right_side, (((0,), (0,)), ((), ())), preferred_element_type=jnp.float32
    )


def contract_cols(left_side, right_side):
    return lax.dot_general(
        left_side, right_side, (((1,), (1,)), ((), ())), preferred_element_type=jnp.float32
    )


def backward_layer(grad_pre, source, adjacent, valid_mask, mixed, weight, going_down):
    row_count = adjacent.shape[0]
    selfrows = source[:row_count]
    grad_weight = jnp.stack([contract_rows(selfrows, grad_pre), contract_rows(mixed, grad_pre)])
    grad_bias = jnp.sum(grad_pre.astype(jnp.float32), axis=0)
    if not going_down:
        return (grad_weight, grad_bias, None)
    weights, counts = mask_counts(valid_mask)
    to_self = contract_cols(grad_pre, weight[0])
    to_mixed = contract_cols(grad_pre, weight[1]) / counts[:, None]
    grad_source = jnp.zeros(source.shape, jnp.float32).at[:row_count].add(to_self)
    for column in range(adjacent.shape[1]):
        grad_source = grad_source.at[adjacent[:, column]].add(
            to_mixed * weights[:, column : column + 1]
        )
    return (grad_weight, grad_bias, grad_source)


def shampoo(master, gradient, left_stat, right_stat, left_root, right_root):
    left_new = 0.5 * left_stat + 0.5 * jnp.einsum(
        "kio,kjo->kij", gradient, gradient, precision=highest
    )
    right_new = 0.5 * right_stat + 0.5 * jnp.einsum(
        "kio,kip->kop", gradient, gradient, precision=highest
    )
    direction = jnp.einsum("kij,kjo->kio", left_root, gradient, precision=highest)
    direction = jnp.einsum("kio,kop->kip", direction, right_root, precision=highest)
    updated = master - 1.0 * direction
    return (updated, updated.astype(jnp.bfloat16), left_new, right_new)


def adamw(bias_row, gradient, moment_a, moment_b, step_count):
    first_new = 0.9 * moment_a + 0.1 * gradient
    second_new = 0.95 * moment_b + 0.05 * gradient * gradient
    stepped = step_count.astype(jnp.float32)
    first_hat = first_new / (1.0 - 0.9**stepped)
    second_hat = second_new / (1.0 - 0.95**stepped)
    bias_new = bias_row - 0.1 * (first_hat / (jnp.sqrt(second_hat) + 1e-08) + 0.01 * bias_row)
    return (bias_new, first_new, second_new)


def body(
    features,
    requests,
    adjacent_one,
    adjacent_two,
    adjacent_three,
    valid_one,
    valid_two,
    valid_three,
    labels,
    labelled,
    weights_in,
    weights_mid,
    weights_out,
    biases,
    moment_one,
    moment_two,
    step_count,
    left_in,
    left_mid,
    left_out,
    right_in,
    right_mid,
    right_out,
    invleft_in,
    invleft_mid,
    invleft_out,
    invright_in,
    invright_mid,
    invright_out,
):
    pulled = pull_features(features, requests)
    masters = (weights_in, weights_mid, weights_out)
    lowered = [item.astype(jnp.bfloat16) for item in masters]
    widths = [item.shape[2] for item in masters]
    offsets = [0, widths[0], widths[0] + widths[1]]
    bias_rows = [biases[offsets[which] : offsets[which] + widths[which]] for which in range(3)]
    links = ((adjacent_one, valid_one), (adjacent_two, valid_two), (adjacent_three, valid_three))
    sources = [pulled]
    mixes = []
    preacts = []
    for layer_num in range(3):
        preact, mixed = forward_layer(
            sources[-1],
            links[layer_num][0],
            links[layer_num][1],
            lowered[layer_num],
            bias_rows[layer_num],
        )
        mixes.append(mixed)
        preacts.append(preact)
        if layer_num < 2:
            sources.append(jax.nn.silu(preact).astype(jnp.bfloat16))
    marked = labelled.astype(jnp.float32)
    log_total = jax.nn.logsumexp(preact, axis=1)
    onehot = (labels[:, None] == jnp.arange(preact.shape[1], dtype=jnp.int32)[None, :]).astype(
        jnp.float32
    )
    picked = jnp.sum(preact * onehot, axis=1)
    loss_sum = jnp.sum(marked * (log_total - picked))
    grad_pre = (marked[:, None] * (jnp.exp(preact - log_total[:, None]) - onehot)).astype(
        jnp.bfloat16
    )
    grad_weights = [None, None, None]
    grad_biases = [None, None, None]
    for layer_num in (2, 1, 0):
        grad_weight, grad_bias, grad_source = backward_layer(
            grad_pre,
            sources[layer_num],
            links[layer_num][0],
            links[layer_num][1],
            mixes[layer_num],
            lowered[layer_num],
            layer_num > 0,
        )
        grad_weights[layer_num] = grad_weight
        grad_biases[layer_num] = grad_bias
        if layer_num > 0:
            grad_pre = (grad_source * silu_slope(preacts[layer_num - 1])).astype(jnp.bfloat16)
    local_count = jnp.sum(marked)
    grad_in, grad_mid, grad_out, grad_bias_all, loss_total, counted = lax.psum(
        (
            grad_weights[0],
            grad_weights[1],
            grad_weights[2],
            jnp.concatenate(grad_biases),
            loss_sum,
            local_count,
        ),
        ("hst", "dev"),
    )
    loss = loss_total / counted
    out_in = shampoo(weights_in, grad_in / counted, left_in, right_in, invleft_in, invright_in)
    out_mid = shampoo(
        weights_mid, grad_mid / counted, left_mid, right_mid, invleft_mid, invright_mid
    )
    out_out = shampoo(
        weights_out, grad_out / counted, left_out, right_out, invleft_out, invright_out
    )
    bias_new, first_new, second_new = adamw(
        biases, grad_bias_all / counted, moment_one, moment_two, step_count
    )
    return (
        loss,
        out_in[0],
        out_mid[0],
        out_out[0],
        out_in[1],
        out_mid[1],
        out_out[1],
        out_in[2],
        out_mid[2],
        out_out[2],
        out_in[3],
        out_mid[3],
        out_out[3],
        bias_new,
        first_new,
        second_new,
    )


def solution(mesh):
    placed = (
        P(("hst", "dev"), None),
        P(("hst", "dev"), None),
        P(("hst", "dev"), None),
        P(("hst", "dev"), None),
        P(("hst", "dev"), None),
        P(("hst", "dev"), None),
        P(("hst", "dev"), None),
        P(("hst", "dev"), None),
        P(("hst", "dev")),
        P(("hst", "dev")),
        P(),
        P(),
        P(),
        P(),
        P(),
        P(),
        P(),
        P(),
        P(),
        P(),
        P(),
        P(),
        P(),
        P(),
        P(),
        P(),
        P(),
        P(),
        P(),
    )
    return jax.shard_map(
        body,
        mesh=mesh,
        in_specs=placed,
        out_specs=(P(), P(), P(), P(), P(), P(), P(), P(), P(), P(), P(), P(), P(), P(), P(), P()),
        check_vma=False,
    )
```

profile of v0, /device:TPU:0, one launch (start us, length us, event | category | flops | bytes accessed | tf_op | source)
XLA Modules:
  0.0 596.3 jit_solution(15780768578314852755)
XLA Ops:
  8.6 7.3 %all-to-all-start = ((s32[32,1,256]{2,1,0:T(1,128)}), s32[32,1,256]{2,1,0:T(1,128)S(1)}, u32[]{:S(2)}, u32[]{:S(2)}) async-start(s32[32,1,256]{2,1,0:T(1,128)} %all_to_all.11), calls=%async_computation | async-start | bytes 65536 | tf_op jit(solution)/shard_map/all_to_all | solution.py:12
  25.8 31.4 %gather_fusion = bf16[8192,128]{1,0:T(8,128)(2,1)} fusion(f32[16384,128]{1,0:T(8,128)} %param.33, s32[8192]{0:T(1024)S(1)} %broadcast_clamp_fusion), kind=kCustom, calls=%fused_computation | custom fusion | bytes 4227072 | tf_op jit(solution)/shard_map/gather | solution.py:11
  57.2 5.8 all-to-all-start.1
  68.3 3.2 fusion.66
  78.3 2.8 slice_reduce_fusion.14
  83.9 29.2 %all-to-all-done.1 = bf16[32,256,128]{2,1,0:T(8,128)(2,1)S(1)} async-done(((bf16[32,256,128]{2,1,0:T(8,128)(2,1)}), bf16[32,256,128]{2,1,0:T(8,128)(2,1)S(1)}, u32[]{:S(2)}, u32[]{:S(2)}) %all-to-all-start.1) | async-done | bytes 2097184 | tf_op jit(solution)/shard_map/all_to_all | solution.py:14
  113.1 10.9 %gather_fusion.15 = bf16[4224,128]{1,0:T(8,128)(2,1)} fusion(bf16[8192,128]{1,0:T(8,128)(2,1)S(1)} %bitcast.89, s32[5120]{0:T(1024)} %get-tuple-element.182), kind=kCustom, calls=%fused_computation.15 | custom fusion | bytes 2179584 | tf_op jit(solution)/shard_map/gather | solution.py:29
  124.0 10.5 %gather_fusion.14 = bf16[4224,128]{1,0:T(8,128)(2,1)} fusion(bf16[8192,128]{1,0:T(8,128)(2,1)S(1)} %bitcast.90, s32[5120]{0:T(1024)} %get-tuple-element.183), kind=kCustom, calls=%fused_computation.14 | custom fusion | bytes 2179584 | tf_op jit(solution)/shard_map/gather | solution.py:29
  134.6 9.6 %gather_fusion.13 = bf16[4224,128]{1,0:T(8,128)(2,1)} fusion(bf16[8192,128]{1,0:T(8,128)(2,1)S(1)} %bitcast.91, s32[5120]{0:T(1024)S(1)} %copy-done.25), kind=kCustom, calls=%fused_computation.13 | custom fusion | bytes 2179584 | tf_op jit(solution)/shard_map/gather | solution.py:29
  144.1 9.6 %gather_fusion.12 = bf16[4224,128]{1,0:T(8,128)(2,1)} fusion(bf16[8192,128]{1,0:T(8,128)(2,1)S(1)} %bitcast.92, s32[5120]{0:T(1024)S(1)} %get-tuple-element.185), kind=kCustom, calls=%fused_computation.12 | custom fusion | bytes 2179584 | tf_op jit(solution)/shard_map/gather | solution.py:29
  153.7 10.5 %gather_fusion.11 = bf16[4224,128]{1,0:T(8,128)(2,1)} fusion(bf16[8192,128]{1,0:T(8,128)(2,1)S(1)} %bitcast.93, s32[5120]{0:T(1024)} %get-tuple-element.186), kind=kCustom, calls=%fused_computation.11 | custom fusion | bytes 2179584 | tf_op jit(solution)/shard_map/gather | solution.py:29
  164.2 9.6 %gather_fusion.10 = bf16[4224,128]{1,0:T(8,128)(2,1)} fusion(bf16[8192,128]{1,0:T(8,128)(2,1)S(1)} %bitcast.94, s32[5120]{0:T(1024)S(1)} %copy-done.20), kind=kCustom, calls=%fused_computation.10 | custom fusion | bytes 2179584 | tf_op jit(solution)/shard_map/gather | solution.py:29
  173.8 9.6 %gather_fusion.9 = bf16[4224,128]{1,0:T(8,128)(2,1)} fusion(bf16[8192,128]{1,0:T(8,128)(2,1)S(1)} %bitcast.95, s32[5120]{0:T(1024)S(1)} %copy-done.26), kind=kCustom, calls=%fused_computation.9 | custom fusion | bytes 2179584 | tf_op jit(solution)/shard_map/gather | solution.py:29
  183.4 9.6 %gather_fusion.8 = bf16[4224,128]{1,0:T(8,128)(2,1)} fusion(bf16[8192,128]{1,0:T(8,128)(2,1)S(1)} %bitcast.96, s32[5120]{0:T(1024)S(1)} %copy-done.21), kind=kCustom, calls=%fused_computation.8 | custom fusion | bytes 2179584 | tf_op jit(solution)/shard_map/gather | solution.py:29
  193.0 9.5 %gather_fusion.7 = bf16[4224,128]{1,0:T(8,128)(2,1)} fusion(bf16[8192,128]{1,0:T(8,128)(2,1)S(1)} %bitcast.97, s32[5120]{0:T(1024)S(1)} %copy-done.27), kind=kCustom, calls=%fused_computation.7 | custom fusion | bytes 2179584 | tf_op jit(solution)/shard_map/gather | solution.py:29
  202.5 9.6 %gather_fusion.6 = bf16[4224,128]{1,0:T(8,128)(2,1)} fusion(bf16[8192,128]{1,0:T(8,128)(2,1)S(1)} %bitcast.98, s32[5120]{0:T(1024)S(1)} %copy-done.22), kind=kCustom, calls=%fused_computation.6 | custom fusion | bytes 2179584 | tf_op jit(solution)/shard_map/gather | solution.py:29
  212.1 9.6 %gather_fusion.5 = bf16[4224,128]{1,0:T(8,128)(2,1)} fusion(bf16[8192,128]{1,0:T(8,128)(2,1)S(1)} %bitcast.99, s32[5120]{0:T(1024)S(1)} %copy-done.28), kind=kCustom, calls=%fused_computation.5 | custom fusion | bytes 2179584 | tf_op jit(solution)/shard_map/gather | solution.py:29
  221.7 9.6 %gather_fusion.4 = bf16[4224,128]{1,0:T(8,128)(2,1)} fusion(bf16[8192,128]{1,0:T(8,128)(2,1)S(1)} %bitcast.100, s32[5120]{0:T(1024)S(1)} %copy-done.23), kind=kCustom, calls=%fused_computation.4 | custom fusion | bytes 2179584 | tf_op jit(solution)/shard_map/gather | solution.py:29
  231.3 9.6 %gather_fusion.3 = bf16[4224,128]{1,0:T(8,128)(2,1)} fusion(bf16[8192,128]{1,0:T(8,128)(2,1)S(1)} %bitcast.101, s32[5120]{0:T(1024)S(1)} %copy-done.29), kind=kCustom, calls=%fused_computation.3 | custom fusion | bytes 2179584 | tf_op jit(solution)/shard_map/gather | solution.py:29
  240.9 9.6 %gather_fusion.2 = bf16[4224,128]{1,0:T(8,128)(2,1)} fusion(bf16[8192,128]{1,0:T(8,128)(2,1)S(1)} %bitcast.102, s32[5120]{0:T(1024)S(1)} %copy-done.24), kind=kCustom, calls=%fused_computation.2 | custom fusion | bytes 2179584 | tf_op jit(solution)/shard_map/gather | solution.py:29
  250.5 9.6 %gather_fusion.1 = bf16[4224,128]{1,0:T(8,128)(2,1)} fusion(bf16[8192,128]{1,0:T(8,128)(2,1)S(1)} %bitcast.103, s32[5120]{0:T(1024)S(1)} %copy-done.30), kind=kCustom, calls=%fused_computation.1 | custom fusion | bytes 2179584 | tf_op jit(solution)/shard_map/gather | solution.py:29
  262.6 13.4 %divide_convert_fusion = bf16[4224,128]{1,0:T(8,128)(2,1)S(1)} fusion(bf16[4224,128]{1,0:T(8,128)(2,1)S(1)} %copy-done.1, bf16[4224,128]{1,0:T(8,128)(2,1)S(1)} %copy-done.2, bf16[4224,128]{1,0:T(8,128)(2,1)S(1)} %copy-done.3, bf16[4224,128]{1,0:T(8,128)(2,1)S(1)} %copy-done.4, bf16[4224,128]{1,0:T(8,128)(2,1)S(1)} %copy-done.5, ...), kind=kLoop, calls=%fused_computation.52 | loop fusion | flops 24870912 | bytes 17571840 | tf_op jit(solution)/shard_map/convert_element_type | solution.py:31
  276.0 4.0 multiply_convert_fusion.1
  280.0 3.6 gather_fusion.25
  283.6 4.1 gather_fusion.24
  287.7 4.1 gather_fusion.23
  291.7 4.2 gather_fusion.22
  296.0 4.1 gather_fusion.21
  300.0 4.1 gather_fusion.20
  304.1 4.1 gather_fusion.19
  308.2 4.1 gather_fusion.18
  312.3 4.1 gather_fusion.17
  316.4 4.1 gather_fusion.16
  353.9 7.1 %scatter_custom_fusion.5 = f32[4224,256]{1,0:T(8,128)} fusion(f32[4224,256]{1,0:T(8,128)} %scatter-add.121, s32[384]{0:T(512)} %copy-done.68, f32[384,256]{1,0:T(8,128)S(1)} %convolution_divide_fusion, f32[384]{0:T(512)S(1)} %copy-done.42), kind=kCustom, calls=%fused_computation.103 | custom fusion | flops 196608 | bytes 4720128 | tf_op jit(solution)/shard_map/scatter-add | solution.py:70
  361.0 6.9 %scatter_custom_fusion.6 = f32[4224,256]{1,0:T(8,128)} fusion(f32[4224,256]{1,0:T(8,128)} %scatter_custom_fusion.5, s32[384]{0:T(512)} %copy-done.67, f32[384,256]{1,0:T(8,128)S(1)} %convolution_divide_fusion, f32[384]{0:T(512)S(1)} %copy-done.40), kind=kCustom, calls=%fused_computation.101 | custom fusion | flops 196608 | bytes 4720128 | tf_op jit(solution)/shard_map/scatter-add | solution.py:70
  367.9 6.9 %scatter_custom_fusion.7 = f32[4224,256]{1,0:T(8,128)} fusion(f32[4224,256]{1,0:T(8,128)} %scatter_custom_fusion.6, s32[384]{0:T(512)} %copy-done.66, f32[384,256]{1,0:T(8,128)S(1)} %convolution_divide_fusion, f32[384]{0:T(512)S(1)} %copy-done.38), kind=kCustom, calls=%fused_computation.99 | custom fusion | flops 196608 | bytes 4720128 | tf_op jit(solution)/shard_map/scatter-add | solution.py:70
  374.7 6.9 %scatter_custom_fusion.8 = f32[4224,256]{1,0:T(8,128)} fusion(f32[4224,256]{1,0:T(8,128)} %scatter_custom_fusion.7, s32[384]{0:T(512)} %copy-done.65, f32[384,256]{1,0:T(8,128)S(1)} %convolution_divide_fusion, f32[384]{0:T(512)S(1)} %copy-done.37), kind=kCustom, calls=%fused_computation.97 | custom fusion | flops 196608 | bytes 4720128 | tf_op jit(solution)/shard_map/scatter-add | solution.py:70
  381.6 6.9 %scatter_custom_fusion.9 = f32[4224,256]{1,0:T(8,128)} fusion(f32[4224,256]{1,0:T(8,128)} %scatter_custom_fusion.8, s32[384]{0:T(512)} %copy-done.64, f32[384,256]{1,0:T(8,128)S(1)} %convolution_divide_fusion, f32[384]{0:T(512)S(1)} %copy-done.36), kind=kCustom, calls=%fused_computation.95 | custom fusion | flops 196608 | bytes 4720128 | tf_op jit(solution)/shard_map/scatter-add | solution.py:70
  388.4 6.9 %scatter_custom_fusion.10 = f32[4224,256]{1,0:T(8,128)} fusion(f32[4224,256]{1,0:T(8,128)} %scatter_custom_fusion.9, s32[384]{0:T(512)} %copy-done.63, f32[384,256]{1,0:T(8,128)S(1)} %convolution_divide_fusion, f32[384]{0:T(512)S(1)} %copy-done.35), kind=kCustom, calls=%fused_computation.93 | custom fusion | flops 196608 | bytes 4720128 | tf_op jit(solution)/shard_map/scatter-add | solution.py:70
  395.3 7.3 %scatter_custom_fusion.11 = f32[4224,256]{1,0:T(8,128)} fusion(f32[4224,256]{1,0:T(8,128)} %scatter_custom_fusion.10, s32[384]{0:T(512)} %copy-done.62, f32[384,256]{1,0:T(8,128)S(1)} %convolution_divide_fusion, f32[384]{0:T(512)S(1)} %copy-done.34), kind=kCustom, calls=%fused_computation.91 | custom fusion | flops 196608 | bytes 4720128 | tf_op jit(solution)/shard_map/scatter-add | solution.py:70
  402.5 6.9 %scatter_custom_fusion.12 = f32[4224,256]{1,0:T(8,128)} fusion(f32[4224,256]{1,0:T(8,128)} %scatter_custom_fusion.11, s32[384]{0:T(512)} %copy-done.61, f32[384,256]{1,0:T(8,128)S(1)} %convolution_divide_fusion, f32[384]{0:T(512)S(1)} %copy-done.33), kind=kCustom, calls=%fused_computation.89 | custom fusion | flops 196608 | bytes 4720128 | tf_op jit(solution)/shard_map/scatter-add | solution.py:70
  409.4 6.9 %scatter_custom_fusion.13 = f32[4224,256]{1,0:T(8,128)} fusion(f32[4224,256]{1,0:T(8,128)} %scatter_custom_fusion.12, s32[384]{0:T(512)} %copy-done.60, f32[384,256]{1,0:T(8,128)S(1)} %convolution_divide_fusion, f32[384]{0:T(512)S(1)} %copy-done.32), kind=kCustom, calls=%fused_computation.87 | custom fusion | flops 196608 | bytes 4720128 | tf_op jit(solution)/shard_map/scatter-add | solution.py:70
  416.2 6.9 %scatter_custom_fusion.14 = f32[4224,256]{1,0:T(8,128)} fusion(f32[4224,256]{1,0:T(8,128)} %scatter_custom_fusion.13, s32[384]{0:T(512)} %copy-done.59, f32[384,256]{1,0:T(8,128)S(1)} %convolution_divide_fusion, f32[384]{0:T(512)S(1)} %get-tuple-element.121), kind=kCustom, calls=%fused_computation.85 | custom fusion | flops 196608 | bytes 4720128 | tf_op jit(solution)/shard_map/scatter-add | solution.py:70
  423.1 4.4 convert_reduce_fusion
  432.9 37.8 %all-reduce.2 = (f32[]{:T(128)}, f32[]{:T(128)}, f32[684]{0:T(1024)S(1)}) all-reduce(f32[]{:T(128)} %get-tuple-element.141, f32[]{:T(128)} %get-tuple-element.140, f32[684]{0:T(1024)S(1)} %pad_maximum_fusion.3), channel_id=1, replica_groups=mesh['hst'=4,'dev'=8] {'hst','dev'}, use_global_device_ids=true, to_apply=%region_7.8 | all-reduce | flops 686 | bytes 5488 | tf_op jit(solution)/shard_map/psum | solution.py:179
  473.3 88.9 %all-reduce.6.cloned.1.call-done = (f32[2,128,256]{2,1,0:T(8,128)}, f32[2,256,256]{2,1,0:T(8,128)}, f32[2,256,172]{1,2,0:T(8,128)}) async-done(((f32[2,128,256]{2,1,0:T(8,128)}, f32[2,256,256]{2,1,0:T(8,128)}, f32[2,256,172]{1,2,0:T(8,128)}), (f32[2,128,256]{2,1,0:T(8,128)}, f32[2,256,256]{2,1,0:T(8,128)}, f32[2,256,172]{1,2,0:T(8,128)})) %all-reduce.6.cloned.1.call-update) | async-done | bytes 1138704 | tf_op jit(solution)/shard_map/psum | solution.py:179
  562.2 2.8 fusion.7
  567.1 3.2 fusion.3
  (273 shorter events, 87.4 us)
Async XLA Ops:
  7.2 579.4 %copy-start = (f32[2,256,256]{2,1,0:T(8,128)S(1)}, f32[2,256,256]{2,1,0:T(8,128)}, u32[]{:S(2)}) copy-start(f32[2,256,256]{2,1,0:T(8,128)} %param.60) | copy-start | bytes 1572868
  8.6 17.1 %all-to-all-start = ((s32[32,1,256]{2,1,0:T(1,128)}), s32[32,1,256]{2,1,0:T(1,128)S(1)}, u32[]{:S(2)}, u32[]{:S(2)}) async-start(s32[32,1,256]{2,1,0:T(1,128)} %all_to_all.11), calls=%async_computation | async-start | bytes 65536 | tf_op jit(solution)/shard_map/all_to_all | solution.py:12
  57.2 7.9 %copy-start.47 = (s32[384,10]{0,1:T(8,128)S(1)}, s32[384,10]{0,1:T(8,128)}, u32[]{:S(2)}) copy-start(s32[384,10]{0,1:T(8,128)} %param.36) | copy-start | bytes 46084
  57.2 15.0 %copy-start.19 = (s32[384,10]{0,1:T(8,128)S(1)}, s32[384,10]{0,1:T(8,128)}, u32[]{:S(2)}) copy-start(s32[384,10]{0,1:T(8,128)} %param.39) | copy-start | bytes 46084
  57.2 21.0 %copy-start.10 = (s32[4224,15]{0,1:T(8,128)S(1)}, s32[4224,15]{0,1:T(8,128)}, u32[]{:S(2)}) copy-start(s32[4224,15]{0,1:T(8,128)} %param.38) | copy-start | bytes 760324
  57.2 55.9 %all-to-all-start.1 = ((bf16[32,256,128]{2,1,0:T(8,128)(2,1)}), bf16[32,256,128]{2,1,0:T(8,128)(2,1)S(1)}, u32[]{:S(2)}, u32[]{:S(2)}) async-start(bf16[32,256,128]{2,1,0:T(8,128)(2,1)} %bitcast.106), calls=%async_computation.1 | async-start | bytes 4194304 | tf_op jit(solution)/shard_map/all_to_all | solution.py:14
  63.1 499.2 %all-reduce.6.cloned.1.call-start = ((), (), s32[]{:S(2)}) async-start(), calls=%async_computation.2 | async-start | bytes 2293760 | tf_op jit(solution)/shard_map/psum | solution.py:179
  63.1 19.0 %copy-start.44 = (f32[684]{0:T(1024)S(1)}, f32[684]{0:T(1024)}, u32[]{:S(2)}) copy-start(f32[684]{0:T(1024)} %param.46) | copy-start | bytes 8212
  63.1 19.6 %copy-start.46 = (f32[64,5]{0,1:T(8,128)S(1)}, f32[64,5]{0,1:T(8,128)}, u32[]{:S(2)}) copy-start(f32[64,5]{0,1:T(8,128)} %convert_element_type.201) | copy-start | bytes 3844
  124.0 10.5 %copy-start.25 = (s32[5120]{0:T(1024)S(1)}, s32[5120]{0:T(1024)}, u32[]{:S(2)}) copy-start(s32[5120]{0:T(1024)} %get-tuple-element.184) | copy-start | bytes 61444
  153.7 10.5 %copy-start.20 = (s32[5120]{0:T(1024)S(1)}, s32[5120]{0:T(1024)}, u32[]{:S(2)}) copy-start(s32[5120]{0:T(1024)} %get-tuple-element.187) | copy-start | bytes 61444
  164.2 9.6 %copy-start.26 = (s32[5120]{0:T(1024)S(1)}, s32[5120]{0:T(1024)}, u32[]{:S(2)}) copy-start(s32[5120]{0:T(1024)} %get-tuple-element.188) | copy-start | bytes 61444
  173.8 9.6 %copy-start.21 = (s32[5120]{0:T(1024)S(1)}, s32[5120]{0:T(1024)}, u32[]{:S(2)}) copy-start(s32[5120]{0:T(1024)} %get-tuple-element.189) | copy-start | bytes 61444
  183.4 9.6 %copy-start.27 = (s32[5120]{0:T(1024)S(1)}, s32[5120]{0:T(1024)}, u32[]{:S(2)}) copy-start(s32[5120]{0:T(1024)} %get-tuple-element.190) | copy-start | bytes 61444
  193.0 9.6 %copy-start.22 = (s32[5120]{0:T(1024)S(1)}, s32[5120]{0:T(1024)}, u32[]{:S(2)}) copy-start(s32[5120]{0:T(1024)} %get-tuple-element.191) | copy-start | bytes 61444
  202.5 9.6 %copy-start.28 = (s32[5120]{0:T(1024)S(1)}, s32[5120]{0:T(1024)}, u32[]{:S(2)}) copy-start(s32[5120]{0:T(1024)} %get-tuple-element.192) | copy-start | bytes 61444
  212.1 9.6 %copy-start.23 = (s32[5120]{0:T(1024)S(1)}, s32[5120]{0:T(1024)}, u32[]{:S(2)}) copy-start(s32[5120]{0:T(1024)} %get-tuple-element.193) | copy-start | bytes 61444
  221.7 9.6 %copy-start.29 = (s32[5120]{0:T(1024)S(1)}, s32[5120]{0:T(1024)}, u32[]{:S(2)}) copy-start(s32[5120]{0:T(1024)} %get-tuple-element.194) | copy-start | bytes 61444
  231.3 9.6 %copy-start.24 = (s32[5120]{0:T(1024)S(1)}, s32[5120]{0:T(1024)}, u32[]{:S(2)}) copy-start(s32[5120]{0:T(1024)} %get-tuple-element.195) | copy-start | bytes 61444
  240.9 9.6 %copy-start.30 = (s32[5120]{0:T(1024)S(1)}, s32[5120]{0:T(1024)}, u32[]{:S(2)}) copy-start(s32[5120]{0:T(1024)} %pad_clamp_fusion.14) | copy-start | bytes 61444
  276.0 7.6 %copy-start.56 = (s32[1024]{0:T(1024)S(1)}, s32[1024]{0:T(1024)}, u32[]{:S(2)}) copy-start(s32[1024]{0:T(1024)} %get-tuple-element.197) | copy-start | bytes 12292
  280.0 7.7 %copy-start.55 = (s32[1024]{0:T(1024)S(1)}, s32[1024]{0:T(1024)}, u32[]{:S(2)}) copy-start(s32[1024]{0:T(1024)} %get-tuple-element.198) | copy-start | bytes 12292
  283.6 8.2 %copy-start.54 = (s32[1024]{0:T(1024)S(1)}, s32[1024]{0:T(1024)}, u32[]{:S(2)}) copy-start(s32[1024]{0:T(1024)} %get-tuple-element.199) | copy-start | bytes 12292
  287.7 8.3 %copy-start.53 = (s32[1024]{0:T(1024)S(1)}, s32[1024]{0:T(1024)}, u32[]{:S(2)}) copy-start(s32[1024]{0:T(1024)} %get-tuple-element.200) | copy-start | bytes 12292
  291.7 8.3 %copy-start.52 = (s32[1024]{0:T(1024)S(1)}, s32[1024]{0:T(1024)}, u32[]{:S(2)}) copy-start(s32[1024]{0:T(1024)} %get-tuple-element.201) | copy-start | bytes 12292
  296.0 8.2 %copy-start.51 = (s32[1024]{0:T(1024)S(1)}, s32[1024]{0:T(1024)}, u32[]{:S(2)}) copy-start(s32[1024]{0:T(1024)} %get-tuple-element.202) | copy-start | bytes 12292
  300.0 8.1 %copy-start.50 = (s32[1024]{0:T(1024)S(1)}, s32[1024]{0:T(1024)}, u32[]{:S(2)}) copy-start(s32[1024]{0:T(1024)} %get-tuple-element.203) | copy-start | bytes 12292
  304.1 8.2 %copy-start.49 = (s32[1024]{0:T(1024)S(1)}, s32[1024]{0:T(1024)}, u32[]{:S(2)}) copy-start(s32[1024]{0:T(1024)} %get-tuple-element.204) | copy-start | bytes 12292
  308.2 8.2 %copy-start.48 = (s32[1024]{0:T(1024)S(1)}, s32[1024]{0:T(1024)}, u32[]{:S(2)}) copy-start(s32[1024]{0:T(1024)} %get-tuple-element.205) | copy-start | bytes 12292
  312.2 9.3 %copy-start.32 = (f32[384]{0:T(512)S(1)}, f32[384]{0:T(512)}, u32[]{:S(2)}) copy-start(f32[384]{0:T(512)} %get-tuple-element.122) | copy-start | bytes 4612
  312.2 9.4 %copy-start.33 = (f32[384]{0:T(512)S(1)}, f32[384]{0:T(512)}, u32[]{:S(2)}) copy-start(f32[384]{0:T(512)} %get-tuple-element.123) | copy-start | bytes 4612
  312.2 9.4 %copy-start.34 = (f32[384]{0:T(512)S(1)}, f32[384]{0:T(512)}, u32[]{:S(2)}) copy-start(f32[384]{0:T(512)} %get-tuple-element.124) | copy-start | bytes 4612
  312.2 9.4 %copy-start.35 = (f32[384]{0:T(512)S(1)}, f32[384]{0:T(512)}, u32[]{:S(2)}) copy-start(f32[384]{0:T(512)} %get-tuple-element.125) | copy-start | bytes 4612
  312.2 9.4 %copy-start.36 = (f32[384]{0:T(512)S(1)}, f32[384]{0:T(512)}, u32[]{:S(2)}) copy-start(f32[384]{0:T(512)} %get-tuple-element.126) | copy-start | bytes 4612
  312.3 9.4 %copy-start.37 = (f32[384]{0:T(512)S(1)}, f32[384]{0:T(512)}, u32[]{:S(2)}) copy-start(f32[384]{0:T(512)} %get-tuple-element.127) | copy-start | bytes 4612
  312.3 9.4 %copy-start.38 = (f32[384]{0:T(512)S(1)}, f32[384]{0:T(512)}, u32[]{:S(2)}) copy-start(f32[384]{0:T(512)} %get-tuple-element.128) | copy-start | bytes 4612
  312.3 9.4 %copy-start.39 = (f32[384]{0:T(512)S(1)}, f32[384]{0:T(512)}, u32[]{:S(2)}) copy-start(f32[384]{0:T(512)} %get-tuple-element.129) | copy-start | bytes 4612
  312.3 9.4 %copy-start.41 = (f32[384]{0:T(512)S(1)}, f32[384]{0:T(512)}, u32[]{:S(2)}) copy-start(f32[384]{0:T(512)} %get-tuple-element.120) | copy-start | bytes 4612
  312.3 9.4 %copy-start.58 = (f32[384]{0:T(512)S(1)}, f32[384]{0:T(512)}, u32[]{:S(2)}) copy-start(f32[384]{0:T(512)} %broadcast_maximum_fusion.1) | copy-start | bytes 4612
  323.8 9.0 %copy-start.14 = (bf16[384,256]{1,0:T(8,128)(2,1)}, bf16[384,256]{1,0:T(8,128)(2,1)S(1)}, u32[]{:S(2)}) copy-start(bf16[384,256]{1,0:T(8,128)(2,1)S(1)} %divide_convert_fusion.1) | copy-start | bytes 589828
  429.7 42.4 %copy-start.45 = (f32[684]{0:T(1024)S(1)}, f32[684]{0:T(1024)}, u32[]{:S(2)}) copy-start(f32[684]{0:T(1024)} %param.46) | copy-start | bytes 8212
  429.7 42.4 %copy-start.71 = (f32[684]{0:T(1024)S(1)}, f32[684]{0:T(1024)}, u32[]{:S(2)}) copy-start(f32[684]{0:T(1024)} %param.48) | copy-start | bytes 8212
  429.7 42.4 %copy-start.72 = (f32[684]{0:T(1024)S(1)}, f32[684]{0:T(1024)}, u32[]{:S(2)}) copy-start(f32[684]{0:T(1024)} %param.47) | copy-start | bytes 8212
  429.7 132.5 %copy-start.88 = (f32[2,128,128]{2,1,0:T(8,128)S(1)}, f32[2,128,128]{2,1,0:T(8,128)}, u32[]{:S(2)}) copy-start(f32[2,128,128]{2,1,0:T(8,128)} %param.50) | copy-start | bytes 393220
  429.7 135.3 %copy-start.89 = (f32[2,128,128]{2,1,0:T(8,128)S(1)}, f32[2,128,128]{2,1,0:T(8,128)}, u32[]{:S(2)}) copy-start(f32[2,128,128]{2,1,0:T(8,128)} %param.56) | copy-start | bytes 393220
  430.5 136.6 %copy-start.16 = (f32[2,256,256]{2,1,0:T(8,128)S(1)}, f32[2,256,256]{2,1,0:T(8,128)}, u32[]{:S(2)}) copy-start(f32[2,256,256]{2,1,0:T(8,128)} %param.53) | copy-start | bytes 1572868
  432.0 138.2 %copy-start.87 = (f32[2,172,172]{2,0,1:T(2,128)S(1)}, f32[2,172,172]{2,0,1:T(2,128)}, u32[]{:S(2)}) copy-start(f32[2,172,172]{2,0,1:T(2,128)} %param.55) | copy-start | bytes 710020
  562.2 8.1 %copy-start.86 = (f32[2,256,172]{1,2,0:T(8,128)S(1)}, f32[2,256,172]{1,2,0:T(8,128)}, u32[]{:S(2)}) copy-start(f32[2,256,172]{1,2,0:T(8,128)} %get-tuple-element.147) | copy-start | bytes 1056772
  (45 other events, 147.4 us)
Sparse Core Ops, SparseCore 0:
  432.2 129.9 all-reduce.5
where the time goes:
time: 603 us; the launch traced here: 596 us
  local copies, waits for them, and re-layouts  242 us (40%)
  other arithmetic  128 us (21%)
  waiting for transfers between devices  118 us (20%)
  matrix products  38.9 us (6%)
  blocking collectives  37.8 us (6%)
  between operations  18.5 us (3%)
  starting transfers between devices  13.2 us (2%)
    gather x30, local copies, waits for them, and re-layouts, forward_layer(): source[adjacent[:, column]].astype(jnp.float32)  193 us
    psum x1, waiting for transfers between devices, body(): lax.psum((grad_weights[0], grad_weights[1], grad_weights[2], jnp.concaten...  88.9 us
    scatter-add x15, other arithmetic, backward_layer(): grad_source.at[adjacent[:, column]]  75.7 us
    psum x1, blocking collectives, body(): lax.psum((grad_weights[0], grad_weights[1], grad_weights[2], jnp.concaten...  37.8 us
    gather x1, local copies, waits for them, and re-layouts, pull_features(): features[lax.all_to_all(requests, ('hst', 'dev'), split_axis=0, concat_ax...  31.4 us
    all_to_all x1, waiting for transfers between devices, pull_features(): lax.all_to_all(found, ('hst', 'dev'), split_axis=0, concat_axis=0, tiled=...  29.2 us
    convert_element_type x3, other arithmetic, forward_layer(): mixed = (summed / counts[:, None]).astype(jnp.bfloat16)  16.5 us
  transfers between devices with their start and end apart: 3, of which 2 were waited for; matrix products, arithmetic and copies ran while one was open for 5% of the time, Pallas kernels for 0%

commit v1 on v0

v1 whole, which is shorter than its diff:
```python
import functools

import jax
import jax.numpy as jnp
from jax import lax
from jax.experimental import pallas as pl
from jax.experimental.pallas import tpu as pltpu
from jax.sharding import PartitionSpec as P

LANES = 128
SPAN = 256
VMEM_BYTES = 56 << 20
AXES = ("chip", "core", "dev")
PEERS = ("chip", "dev")

smem = pl.BlockSpec(memory_space=pltpu.SMEM)
vmem = pl.BlockSpec(memory_space=pltpu.VMEM)


def up(value, unit):
    return -(-value // unit) * unit


def call(kernel, name, out_shape, in_specs, out_specs, scratch, flops, moved):
    return pl.pallas_call(
        kernel,
        name=name,
        out_shape=out_shape,
        in_specs=in_specs,
        out_specs=out_specs,
        scratch_shapes=scratch,
        compiler_params=pltpu.CompilerParams(vmem_limit_bytes=VMEM_BYTES),
        cost_estimate=pl.CostEstimate(flops=flops, transcendentals=0, bytes_accessed=moved),
    )


def dot(left, right):
    return jnp.dot(left, right, preferred_element_type=jnp.float32)


def dot_rows(left, right):
    return lax.dot_general(
        left, right, (((0,), (0,)), ((), ())), preferred_element_type=jnp.float32
    )


def dot_cols(left, right):
    return lax.dot_general(
        left, right, (((1,), (1,)), ((), ())), preferred_element_type=jnp.float32
    )


def halves(value):
    high = value.astype(jnp.bfloat16)
    return high, (value - high.astype(jnp.float32)).astype(jnp.bfloat16)


def squared(value, size):
    short = size - value.shape[0]
    if short == 0:
        return value
    value = jnp.concatenate([value, jnp.zeros((value.shape[0], short), value.dtype)], axis=1)
    return jnp.concatenate([value, jnp.zeros((short, size), value.dtype)], axis=0)


def clipped_counts(valid):
    return jnp.maximum(jnp.sum(valid.astype(jnp.float32), axis=1, keepdims=True), 1.0)


def pick_kernel(wanted, table, out, rows, *, unroll):
    def body(step, carry):
        base = step * unroll
        for u in range(unroll):
            rows[pl.ds(base + u, 1), :] = table[pl.ds(wanted[base + u], 1), :]
        return carry

    lax.fori_loop(0, out.shape[0] // unroll, body, 0)
    out[...] = rows[...].astype(jnp.bfloat16)


def pick_rows(wanted, table):
    count, width = wanted.shape[0], table.shape[1]
    return call(
        functools.partial(pick_kernel, unroll=32),
        "pick_rows",
        jax.ShapeDtypeStruct((count, width), jnp.bfloat16),
        [smem, vmem],
        vmem,
        [pltpu.VMEM((count, width), jnp.float32)],
        count * width,
        table.size * 4,
    )(wanted, table)


def mean_kernel(slots, valid, source, out, table, total, *, unroll):
    fan, targets = slots.shape
    width = source.shape[1]
    table[0 : source.shape[0], :] = source[...].astype(jnp.float32)
    table[source.shape[0] :, :] = jnp.zeros((8, width), jnp.float32)

    def body(step, carry):
        base = step * unroll
        for u in range(unroll):
            parts = [table[pl.ds(slots[j, base + u], 1), :] for j in range(fan)]
            while len(parts) > 1:
                merged = [parts[k] + parts[k + 1] for k in range(0, len(parts) - 1, 2)]
                parts = merged + parts[len(merged) * 2 :]
            total[pl.ds(base + u, 1), :] = parts[0]
        return carry

    lax.fori_loop(0, targets // unroll, body, 0)
    counts = clipped_counts(valid[...])
    out[0:targets, 0:width] = source[0:targets, :]
    out[0:targets, width : 2 * width] = (total[...] / counts).astype(jnp.bfloat16)
    if out.shape[0] > targets:
        out[targets:, :] = jnp.zeros((out.shape[0] - targets, 2 * width), jnp.bfloat16)


def mean_rows(slots, valid, source, padded):
    fan, targets = slots.shape
    total, width = source.shape
    return call(
        functools.partial(mean_kernel, unroll=8),
        "mean_rows",
        jax.ShapeDtypeStruct((padded, 2 * width), jnp.bfloat16),
        [smem, vmem, vmem],
        vmem,
        [pltpu.VMEM((total + 8, width), jnp.float32), pltpu.VMEM((targets, width), jnp.float32)],
        fan * targets * width,
        total * width * 2,
    )(slots, valid, source)


def link_kernel(names, adjacent, valid, out):
    targets, fan = adjacent.shape
    tile = 32
    blocks = out.shape[0]

    def rows(step, carry):
        first = pl.multiple_of(step * tile, tile)
        here = jnp.where(
            valid[pl.ds(first, tile), :] > 0, adjacent[pl.ds(first, tile), :], -1
        )
        spread = [jnp.broadcast_to(here[:, j : j + 1], (tile, LANES)) for j in range(fan)]
        own = first + lax.broadcasted_iota(jnp.int32, (tile, LANES), 0)

        def columns(block, inner):
            for part in range(SPAN // LANES):
                name = jnp.broadcast_to(
                    names[pl.ds(block * (SPAN // LANES) + part, 1), :], (tile, LANES)
                )
                number = jnp.zeros((tile, LANES), jnp.float32)
                for j in range(fan):
                    number = number + jnp.where(spread[j] == name, 1.0, 0.0)
                lanes = pl.ds(part * LANES, LANES)
                out[block, pl.ds(first, tile), lanes] = number.astype(jnp.bfloat16)
                out[block, pl.ds(targets + first, tile), lanes] = jnp.where(
                    own == name, 1.0, 0.0
                ).astype(jnp.bfloat16)
            return inner

        return lax.fori_loop(0, blocks, columns, carry)

    lax.fori_loop(0, targets // tile, rows, 0)


def link_matrix(names, adjacent, valid):
    blocks = names.size // SPAN
    targets = adjacent.shape[0]
    return call(
        link_kernel,
        "link_matrix",
        jax.ShapeDtypeStruct((blocks, 2 * targets, SPAN), jnp.bfloat16),
        [vmem, vmem, vmem],
        vmem,
        [],
        blocks * targets * SPAN * 30,
        blocks * targets * SPAN * 4,
    )(names, adjacent, valid)


def step_kernel(
    info,
    mixin,
    links,
    valid_two,
    adjacent_three,
    valid_three,
    labels,
    labelled,
    weights_in,
    weights_mid,
    weights_out,
    biases,
    keep,
    send,
    slopes,
    packed,
    sums,
    weight_sums,
    mid_sums,
    tail_sums,
    *,
    classes,
):
    blocks, both, _ = links.shape
    targets = both // 2
    hidden = weights_in.shape[2]
    seeds = labels.shape[0]
    wide = up(classes, LANES)
    core = info[0]
    used = info[1]
    low = jnp.bfloat16

    w_in = weights_in[...].astype(low).reshape(2 * weights_in.shape[1], hidden)
    bias_in = biases[:, 0:hidden]
    bias_mid = biases[:, hidden : 2 * hidden]
    bias_out = jnp.concatenate(
        [
            biases[:, 2 * hidden : 2 * hidden + classes],
            jnp.full((1, wide - classes), -1e30, jnp.float32),
        ],
        axis=1,
    )

    sums[...] = jnp.zeros_like(sums)

    def forward(block, carry):
        rows = pl.ds(pl.multiple_of(block * SPAN, SPAN), SPAN)
        z = dot(mixin[rows, :], w_in) + bias_in
        s = 1.0 / (1.0 + jnp.exp(-z))
        slopes[rows, :] = s * (1.0 + z * (1.0 - s))
        sums[...] += dot(links[block], (z * s).astype(low))
        return carry

    lax.fori_loop(0, used, forward, 0)
    total = sums[...]
    counts_two = clipped_counts(valid_two[...])
    mixed_one = (total[0:targets] / counts_two).astype(low)
    self_one = total[targets:].astype(low)
    w_mid = weights_mid[...].astype(low)
    both_one = jnp.concatenate([self_one, mixed_one], axis=1)
    z = dot(both_one, w_mid.reshape(2 * hidden, hidden)) + bias_mid
    s = 1.0 / (1.0 + jnp.exp(-z))
    slope_mid = s * (1.0 + z * (1.0 - s))
    hidden_two = (z * s).astype(low)

    here = jnp.where(valid_three[...] > 0, adjacent_three[...], -1)
    place = lax.broadcasted_iota(jnp.int32, (seeds, targets), 1)
    number = jnp.zeros((seeds, targets), jnp.float32)
    for j in range(here.shape[1]):
        number = number + jnp.where(here[:, j : j + 1] == place, 1.0, 0.0)
    number = number.astype(low)
    counts_three = clipped_counts(valid_three[...])
    mixed_two = (dot(number, hidden_two) / counts_three).astype(low)
    self_two = hidden_two[0:seeds]
    w_out = jnp.concatenate(
        [
            weights_out[...],
            jnp.zeros((2, weights_out.shape[1], wide - classes), jnp.float32),
        ],
        axis=2,
    ).astype(low)
    both_two = jnp.concatenate([self_two, mixed_two], axis=1)
    logits = dot(both_two, w_out.reshape(2 * hidden, wide)) + bias_out
    top = jnp.max(logits, axis=1, keepdims=True)
    log_total = top + jnp.log(jnp.sum(jnp.exp(logits - top), axis=1, keepdims=True))
    onehot = jnp.where(
        labels[...] == lax.broadcasted_iota(jnp.int32, (seeds, wide), 1), 1.0, 0.0
    )
    marked = labelled[...].astype(jnp.float32)
    picked = jnp.sum(jnp.where(onehot > 0.0, logits, 0.0), axis=1, keepdims=True)
    loss = jnp.sum(marked * (log_total - picked), axis=0, keepdims=True)
    counted = jnp.sum(marked, axis=0, keepdims=True)
    grad_out = (marked * (jnp.exp(logits - log_total) - onehot)).astype(low)

    tail_sums[...] = dot_rows(grad_out[:, LANES:], both_two)
    bias_grad_out = jnp.sum(grad_out.astype(jnp.float32), axis=0, keepdims=True)
    to_self = dot_cols(grad_out, w_out[0])
    spread = (dot_cols(grad_out, w_out[1]) / counts_three).astype(low)
    sums[0:targets, :] = dot_rows(number, spread)
    sums[0:seeds, :] += to_self
    grad_mid = (sums[0:targets, :] * slope_mid).astype(low)

    mid_sums[...] = dot_rows(both_one, grad_mid)
    bias_grad_mid = jnp.sum(grad_mid.astype(jnp.float32), axis=0, keepdims=True)
    down = jnp.concatenate(
        [dot_cols(grad_mid, w_mid[1]) / counts_two, dot_cols(grad_mid, w_mid[0])], axis=0
    )
    spread = down.astype(low)

    weight_sums[...] = jnp.zeros_like(weight_sums)

    def backward(block, bias):
        rows = pl.ds(pl.multiple_of(block * SPAN, SPAN), SPAN)
        grad = (dot_rows(links[block], spread) * slopes[rows, :]).astype(low)
        weight_sums[...] += dot_rows(mixin[rows, :], grad)
        return bias + jnp.sum(grad.astype(jnp.float32), axis=0, keepdims=True)

    bias_grad_in = lax.fori_loop(0, used, backward, jnp.zeros((1, hidden), jnp.float32))

    row = 0
    for part in (weight_sums, mid_sums):
        for column in range(0, hidden, LANES):
            packed[row : row + part.shape[0], :] = part[:, column : column + LANES]
            row += part.shape[0]
    packed[row : row + 2 * hidden, :] = dot_rows(both_two, grad_out[:, 0:LANES])
    row += 2 * hidden
    high_rows = up(classes - LANES, 16)
    for column in range(0, 2 * hidden, LANES):
        packed[row : row + high_rows, :] = tail_sums[0:high_rows, column : column + LANES]
        row += high_rows
    packed[row:, :] = jnp.zeros((packed.shape[0] - row, LANES), jnp.float32)
    lane = lax.broadcasted_iota(jnp.int32, (1, LANES), 1)
    scalars = jnp.where(lane == 0, loss, 0.0) + jnp.where(lane == 1, counted, 0.0)
    extra = [
        item[:, column : column + LANES]
        for item in (bias_grad_in, bias_grad_mid, bias_grad_out)
        for column in range(0, hidden, LANES)
    ] + [scalars, jnp.zeros((1, LANES), jnp.float32)]
    extra = jnp.concatenate(extra, axis=0)
    high = extra.astype(low).astype(jnp.float32)
    packed[packed.shape[0] - 16 :, :] = jnp.concatenate([high, extra - high], axis=0)
    half = keep.shape[0]
    keep[...] = packed[pl.ds(pl.multiple_of(core * half, 16), half), :].astype(low)
    send[...] = packed[pl.ds(pl.multiple_of((1 - core) * half, 16), half), :].astype(low)


def run_step(info, mixin, links, rest, half, classes):
    padded, width = mixin.shape
    hidden = rest[5].shape[2]
    return call(
        functools.partial(step_kernel, classes=classes),
        "step",
        (jax.ShapeDtypeStruct((half, LANES), jnp.bfloat16),) * 2,
        [smem] + [vmem] * 11,
        (vmem, vmem),
        [
            pltpu.VMEM((padded, hidden), jnp.float32),
            pltpu.VMEM((2 * half, LANES), jnp.float32),
            pltpu.VMEM((links.shape[1], hidden), jnp.float32),
            pltpu.VMEM((width, hidden), jnp.float32),
            pltpu.VMEM((2 * hidden, hidden), jnp.float32),
            pltpu.VMEM((up(classes, LANES) - LANES, 2 * hidden), jnp.float32),
        ],
        4 << 30,
        32 << 20,
    )(info, mixin, links, *rest)


def refit(total, rows):
    extra = total[rows - 16 : rows - 8] + total[rows - 8 : rows]
    high = extra.astype(jnp.bfloat16).astype(jnp.float32)
    return jnp.concatenate([high, extra - high], axis=0)


def pair_kernel(info, mine, theirs, out):
    total = mine[...].astype(jnp.float32) + theirs[...].astype(jnp.float32)
    out[...] = total.astype(jnp.bfloat16)

    @pl.when(info[0] == 1)
    def _():
        rows = total.shape[0]
        out[rows - 16 :, :] = refit(total, rows).astype(jnp.bfloat16)


def pair_sum(info, mine, theirs):
    return call(
        pair_kernel,
        "pair_sum",
        jax.ShapeDtypeStruct(mine.shape, jnp.bfloat16),
        [smem, vmem, vmem],
        vmem,
        [],
        mine.size,
        mine.size * 6,
    )(info, mine, theirs)


def spread_kernel(info, pieces, out):
    total = pieces[0].astype(jnp.float32)
    for k in range(1, pieces.shape[0]):
        total = total + pieces[k].astype(jnp.float32)
    rows = total.shape[0]
    fitted = jnp.concatenate([total[0 : rows - 16], refit(total, rows)], axis=0)
    result = jnp.where(info[2] == 1, fitted, total).astype(jnp.bfloat16)
    for k in range(pieces.shape[0]):
        out[k] = result


def spread_sum(info, pieces):
    return call(
        spread_kernel,
        "spread_sum",
        jax.ShapeDtypeStruct(pieces.shape, jnp.bfloat16),
        [smem, vmem],
        vmem,
        [],
        pieces.size,
        pieces.size * 4,
    )(info, pieces)


def update_kernel(
    info,
    fixes,
    mine,
    theirs,
    biases,
    moment_one,
    moment_two,
    *refs,
    classes,
):
    groups = [refs[5 * k : 5 * k + 5] for k in range(3)]
    loss_out = refs[15]
    outs = [refs[16 + 4 * k : 20 + 4 * k] for k in range(3)]
    bias_out, first_out, second_out = refs[28:31]
    packed = refs[31]
    low = jnp.bfloat16
    half = mine.shape[0]
    core = info[0]
    packed[pl.ds(pl.multiple_of(core * half, 16), half), :] = mine[...].astype(jnp.float32)
    packed[pl.ds(pl.multiple_of((1 - core) * half, 16), half), :] = theirs[...].astype(
        jnp.float32
    )
    last = packed.shape[0]
    extra = packed[last - 16 : last - 8, :] + packed[last - 8 :, :]
    counted = extra[6:7, 1:2]
    inverse = 1.0 / counted
    loss_out[...] = extra[6:7, 0:1] / counted

    row = 0
    gradients = []
    for group in range(3):
        depth, hidden = groups[group][0].shape[1:]
        if hidden % LANES == 0:
            parts = []
            for column in range(0, hidden, LANES):
                parts.append(packed[row : row + 2 * depth, :])
                row += 2 * depth
            whole = jnp.concatenate(parts, axis=1)
        else:
            main = packed[row : row + 2 * depth, :]
            row += 2 * depth
            high_rows = up(hidden - LANES, 16)
            tails = []
            for column in range(0, 2 * depth, LANES):
                tail = jnp.concatenate(
                    [
                        packed[row : row + high_rows, :],
                        jnp.zeros((LANES - high_rows, LANES), jnp.float32),
                    ],
                    axis=0,
                )
                tails.append(jnp.transpose(tail))
                row += high_rows
            whole = jnp.concatenate([main, jnp.concatenate(tails, axis=0)], axis=1)
        gradients.append([whole[k * depth : (k + 1) * depth].astype(low) for k in range(2)])

    for group in range(3):
        master, left, right, left_root, right_root = groups[group]
        new_master, copy, new_left, new_right = outs[group]
        depth, hidden = master.shape[1:]
        wide = up(hidden, LANES)
        for k in range(2):
            grad = gradients[group][k]
            scale = 0.5 * inverse * inverse
            new_left[k] = 0.5 * left[k] + scale * dot_cols(grad, grad)
            product = dot_rows(grad, grad)
            new_right[k] = 0.5 * right[k] + scale * product[0:hidden, 0:hidden]
            root = jnp.concatenate(halves(left_root[k]), axis=1)
            middle = dot(root, jnp.concatenate([grad, grad], axis=0))
            mid_high, mid_rest = halves(middle)
            root_high, root_rest = halves(squared(right_root[k], wide))
            way = dot(
                jnp.concatenate([mid_high, mid_high, mid_rest], axis=1),
                jnp.concatenate([root_high, root_rest, root_high], axis=0),
            )[:, 0:hidden]
            fresh = master[k] - inverse * way
            new_master[k] = fresh
            copy[k] = fresh.astype(low)

    size = biases.shape[1]
    grad = jnp.concatenate([extra[k : k + 1, :] for k in range(6)], axis=1)[:, 0:size]
    grad = grad / counted
    first = 0.9 * moment_one[...] + 0.1 * grad
    second = 0.95 * moment_two[...] + 0.05 * grad * grad
    old = biases[...]
    bias_out[...] = old - 0.1 * (
        (first / fixes[0]) / (jnp.sqrt(second / fixes[1]) + 1e-08) + 0.01 * old
    )
    first_out[...] = first
    second_out[...] = second


def run_update(info, fixes, mine, theirs, vectors, groups, classes):
    outs = [jax.ShapeDtypeStruct((1, 1), jnp.float32)]
    flat = []
    for master, left, right, left_root, right_root in groups:
        flat += [master, left, right, left_root, right_root]
        outs += [
            jax.ShapeDtypeStruct(master.shape, jnp.float32),
            jax.ShapeDtypeStruct(master.shape, jnp.bfloat16),
            jax.ShapeDtypeStruct(left.shape, jnp.float32),
            jax.ShapeDtypeStruct(right.shape, jnp.float32),
        ]
    outs += [jax.ShapeDtypeStruct(vectors[0].shape, jnp.float32)] * 3
    return call(
        functools.partial(update_kernel, classes=classes),
        "update",
        tuple(outs),
        [smem, smem] + [vmem] * (5 + 15),
        (vmem,) * len(outs),
        [pltpu.VMEM((2 * mine.shape[0], LANES), jnp.float32)],
        1 << 30,
        10 << 20,
    )(info, fixes, mine, theirs, *vectors, *flat)


def body(
    features,
    requests,
    adjacent_one,
    adjacent_two,
    adjacent_three,
    valid_one,
    valid_two,
    valid_three,
    labels,
    labelled,
    weights_in,
    weights_mid,
    weights_out,
    biases,
    moment_one,
    moment_two,
    step_count,
    left_in,
    left_mid,
    left_out,
    right_in,
    right_mid,
    right_out,
    invleft_in,
    invleft_mid,
    invleft_out,
    invright_in,
    invright_mid,
    invright_out,
    *,
    peers,
):
    width = features.shape[1]
    targets = adjacent_one.shape[0]
    padded = up(targets, SPAN)
    classes = weights_out.shape[2]
    core = lax.axis_index("core")
    own = lax.axis_index(PEERS)

    wanted = lax.all_to_all(requests, AXES, split_axis=0, concat_axis=0, tiled=True)
    found = pick_rows(wanted.reshape(-1), features)
    pulled = lax.all_to_all(
        found.reshape(requests.shape + (width,)), AXES, split_axis=0, concat_axis=0, tiled=True
    ).reshape(-1, width)

    slots = jnp.where(valid_one > 0, adjacent_one, pulled.shape[0]).T
    mixin = mean_rows(slots, valid_one, pulled, padded)
    names = jnp.arange(padded, dtype=jnp.int32).reshape(-1, LANES)
    links = link_matrix(names, adjacent_two, valid_two)

    hidden = weights_in.shape[2]
    rows = 4 * width * (hidden // LANES) // 2 + 2 * weights_mid.shape[1] * (hidden // LANES)
    rows = 2 * width * (hidden // LANES)
    rows += 2 * weights_mid.shape[1] * (hidden // LANES)
    rows += 2 * weights_out.shape[1] + up(classes - LANES, 16) * (2 * hidden // LANES)
    each = up(-(-(rows + 16) // (2 * peers)), 8)
    half = each * peers
    info = jnp.stack(
        [
            core,
            jnp.int32(padded // SPAN),
            ((core == 1) & (own == peers - 1)).astype(jnp.int32),
        ]
    ).astype(jnp.int32)
    keep, send = run_step(
        info,
        mixin,
        links,
        (
            valid_two,
            adjacent_three,
            valid_three,
            labels[:, None],
            labelled[:, None],
            weights_in,
            weights_mid,
            weights_out,
            biases[None, :],
        ),
        half,
        classes,
    )
    swap = [(0, 1), (1, 0)]
    theirs = lax.ppermute(send, "core", swap)
    summed = pair_sum(info, keep, theirs).reshape(peers, each, LANES)
    pieces = lax.all_to_all(summed, PEERS, split_axis=0, concat_axis=0, tiled=True)
    shared = spread_sum(info, pieces)
    mine = lax.all_to_all(shared, PEERS, split_axis=0, concat_axis=0, tiled=True)
    mine = mine.reshape(half, LANES)
    theirs = lax.ppermute(mine, "core", swap)

    stepped = step_count.astype(jnp.float32)
    fixes = jnp.stack([1.0 - 0.9**stepped, 1.0 - 0.95**stepped])
    outs = run_update(
        info,
        fixes,
        mine,
        theirs,
        (biases[None, :], moment_one[None, :], moment_two[None, :]),
        (
            (weights_in, left_in, right_in, invleft_in, invright_in),
            (weights_mid, left_mid, right_mid, invleft_mid, invright_mid),
            (weights_out, left_out, right_out, invleft_out, invright_out),
        ),
        classes,
    )
    groups = [outs[1 + 4 * k : 5 + 4 * k] for k in range(3)]
    return (
        (outs[0].reshape(()),)
        + tuple(groups[k][which] for which in range(4) for k in range(3))
        + tuple(item.reshape(-1) for item in outs[13:16])
    )


def solution(mesh):
    chips, dev = mesh.shape["hst"] // 2, mesh.shape["dev"]
    fine = jax.sharding.Mesh(mesh.devices.reshape(chips, 2, dev), AXES)
    split = P(AXES, None)
    line = P(AXES)
    whole = P()
    return jax.shard_map(
        functools.partial(body, peers=chips * dev),
        mesh=fine,
        in_specs=(split,) * 8 + (line,) * 2 + (whole,) * 19,
        out_specs=(whole,) * 16,
        check_vma=False,
    )
```

time: 603 us -> 239 us (0.40); the launches traced: 596 us -> 238 us
  local copies, waits for them, and re-layouts: 242 us -> 20.3 us
  Pallas kernels: 0 us -> 136 us
  other arithmetic: 128 us -> 6.39 us
  waiting for transfers between devices: 118 us -> 27.7 us
  matrix products: 38.9 us -> 0 us
  between operations: 18.5 us -> 1.55 us
  starting transfers between devices: 13.2 us -> 2.93 us
    gather x31 -> x0, local copies, waits for them, and re-layouts: 224 us -> none  [the longest x30 193 us: forward_layer(): source[adjacent[:, column]].astype(jnp.float32)]
    pallas_call x0 -> x7, Pallas kernels: none -> 136 us  [the longest x1 75.4 us: mean_rows(): call(functools.partial(mean_kernel, unroll=8), 'mean_rows', jax.ShapeDtyp...]
    psum x1 -> x0, waiting for transfers between devices: 88.9 us -> none  [body(): lax.psum((grad_weights[0], grad_weights[1], grad_weights[2], jnp.concaten...]
    scatter-add x15 -> x0, other arithmetic: 75.7 us -> none  [backward_layer(): grad_source.at[adjacent[:, column]]]
    all_to_all x0 -> x3, blocking collectives: none -> 43.3 us  [the longest x1 15.5 us: body(): lax.all_to_all(summed, PEERS, split_axis=0, concat_axis=0, tiled=True)]
    dot_general x28 -> x0, matrix products: 38.9 us -> none  [the longest x3 7.61 us: shampoo(): jnp.einsum('kio,kjo->kij', gradient, gradient, precision=highest)]
    psum x1 -> x0, blocking collectives: 37.8 us -> none  [body(): lax.psum((grad_weights[0], grad_weights[1], grad_weights[2], jnp.concaten...]
    convert_element_type x9 -> x0, other arithmetic: 24 us -> none  [the longest x3 16.5 us: forward_layer(): mixed = (summed / counts[:, None]).astype(jnp.bfloat16)]
  transfers between devices with their start and end apart: 3 -> 3, of which waited for: 2 -> 2; matrix products, arithmetic and copies ran while one was open for 5% -> 6% of each run, Pallas kernels for 0% -> 6%
where the time goes in v1:
time: 239 us; the launch traced here: 238 us
  Pallas kernels  136 us (57%)
  blocking collectives  43.3 us (18%)
  waiting for transfers between devices  27.7 us (12%)
  local copies, waits for them, and re-layouts  20.3 us (8%)
  other arithmetic  6.39 us (3%)
  starting transfers between devices  2.93 us (1%)
    pallas_call x1, Pallas kernels, mean_rows(): call(functools.partial(mean_kernel, unroll=8), 'mean_rows', jax.ShapeDtyp...  75.4 us
    all_to_all x1, waiting for transfers between devices, body(): lax.all_to_all(found.reshape(requests.shape + (width,)), AXES, split_axis...  25.9 us
    pallas_call x1, Pallas kernels, run_step(): call(functools.partial(step_kernel, classes=classes), 'step', (jax.ShapeD...  24.3 us
    unnamed x47, local copies, waits for them, and re-layouts  16.3 us
    all_to_all x1, blocking collectives, body(): lax.all_to_all(summed, PEERS, split_axis=0, concat_axis=0, tiled=True)  15.5 us
    all_to_all x1, blocking collectives, body(): lax.all_to_all(requests, AXES, split_axis=0, concat_axis=0, tiled=True)  14.4 us
    pallas_call x1, Pallas kernels, link_matrix(): call(link_kernel, 'link_matrix', jax.ShapeDtypeStruct((blocks, 2 * target...  13.9 us
    all_to_all x1, blocking collectives, body(): lax.all_to_all(shared, PEERS, split_axis=0, concat_axis=0, tiled=True)  13.5 us
  transfers between devices with their start and end apart: 3, of which 2 were waited for; matrix products, arithmetic and copies ran while one was open for 6% of the time, Pallas kernels for 6%

profile of v1, /device:TPU:0, one launch (start us, length us, event | category | flops | bytes accessed | tf_op | source)
XLA Modules:
  0.0 238.4 jit_solution(13058346000789921472)
XLA Ops:
  0.6 0.8 all_to_all.15
  1.4 14.4 %all_to_all.24 = s32[32,1,256]{2,1,0:T(1,128)} all-to-all(s32[32,1,256]{2,1,0:T(1,128)S(1)} %all_to_all.15), channel_id=1, replica_groups=mesh['chip'=2,'core'=2,'dev'=8] {'chip','core','dev'}, dimensions={0} | all-to-all | bytes 65536 | tf_op jit(solution)/shard_map/all_to_all | solution.py:561
  15.8 12.7 %pick_rows.1 = bf16[8192,128]{1,0:T(8,128)(2,1)} custom-call(s32[8192]{0:T(1024)} %bitcast.19, f32[16384,128]{1,0:T(8,128)} %table.1), custom_call_target="tpu_custom_call" | custom-call | flops 1048576 | bytes 8388608 | tf_op jit(solution)/shard_map/pick_rows/pallas_call | solution.py:83
  28.5 2.9 %all-to-all-start.1 = ((bf16[32,256,128]{2,1,0:T(8,128)(2,1)}), bf16[32,256,128]{2,1,0:T(8,128)(2,1)S(1)}, u32[]{:S(2)}, u32[]{:S(2)}) async-start(bf16[32,256,128]{2,1,0:T(8,128)(2,1)} %bitcast.14), calls=%async_computation.1 | async-start | bytes 4194304 | tf_op jit(solution)/shard_map/all_to_all | solution.py:563
  31.4 0.0 copy-start.9
  31.4 0.0 copy-start.10
  31.4 0.0 copy-start.11
  31.4 0.0 copy-start.12
  31.4 0.0 copy-start.17
  31.4 0.0 copy-start.3
  31.5 2.1 copy.60.valid
  33.6 0.8 copy.61.adjacent
  34.4 0.8 copy.62.valid.valid_two
  35.2 0.7 copy.64.adjacent_three
  35.9 0.7 copy.65.valid_three
  36.6 0.7 copy.66.labels
  37.3 0.7 copy.67.labelled
  38.1 1.0 copy.68.weights_out.refs_10_
  39.1 0.6 broadcast_in_dim.23.biases
  39.7 0.6 multiply_add_fusion.names
  40.3 13.9 %link_matrix.1.links = bf16[17,768,256]{2,1,0:T(8,128)(2,1)} custom-call(s32[34,128]{1,0:T(8,128)} %multiply_add_fusion.names, s32[384,10]{1,0:T(8,128)} %copy.61.adjacent, s32[384,10]{1,0:T(8,128)} %copy.62.valid.valid_two), custom_call_target="tpu_custom_call" | custom-call | flops 50135040 | bytes 6684672 | tf_op jit(solution)/shard_map/link_matrix/pallas_call | solution.py:170
  54.2 0.6 pad_add_fusion.info
  54.8 0.7 select_bitcast_fusion.slots
  55.5 25.9 %all-to-all-done.1 = bf16[32,256,128]{2,1,0:T(8,128)(2,1)S(1)} async-done(((bf16[32,256,128]{2,1,0:T(8,128)(2,1)}), bf16[32,256,128]{2,1,0:T(8,128)(2,1)S(1)}, u32[]{:S(2)}, u32[]{:S(2)}) %all-to-all-start.1) | async-done | bytes 2097184 | tf_op jit(solution)/shard_map/all_to_all | solution.py:563
  81.5 1.4 copy-done
  82.9 75.4 %mean_rows.1.mixin = bf16[4352,256]{1,0:T(8,128)(2,1)} custom-call(s32[15,4224]{1,0:T(8,128)} %select_bitcast_fusion.slots, s32[4224,15]{1,0:T(8,128)} %copy.60.valid, bf16[8192,128]{1,0:T(8,128)(2,1)} %bitcast.15), custom_call_target="tpu_custom_call" | custom-call | flops 8110080 | bytes 2097152 | tf_op jit(solution)/shard_map/mean_rows/pallas_call | solution.py:122
  158.3 24.3 %step.1 = (bf16[1152,128]{1,0:T(8,128)(2,1)}, bf16[1152,128]{1,0:T(8,128)(2,1)}) custom-call(s32[3]{0:T(128)} %pad_add_fusion.info, bf16[4352,256]{1,0:T(8,128)(2,1)} %mean_rows.1.mixin, bf16[17,768,256]{2,1,0:T(8,128)(2,1)} %link_matrix.1.links, s32[384,10]{1,0:T(8,128)} %copy.62.valid.valid_two, s32[64,5]{1,0:T(8,128)} %copy.64.adjacent_three, ...), custom_call_target="tpu_custom_call" | custom-call | flops 4294967296 | bytes 33554432 | tf_op jit(solution)/shard_map/step/pallas_call | solution.py:332
  182.6 0.0 copy-start.5
  182.6 0.1 collective-permute-start
  182.7 1.8 collective-permute-done.theirs
  184.5 0.7 copy-done.7
  185.2 1.8 pair_sum.1
  187.0 15.5 %all_to_all.25.pieces = bf16[16,72,128]{2,1,0:T(8,128)(2,1)} all-to-all(bf16[16,72,128]{2,1,0:T(8,128)(2,1)} %bitcast.18), channel_id=1, replica_groups=mesh['chip'=2,'core'=2,'dev'=8] {'chip','dev'}, dimensions={0} | all-to-all | bytes 589824 | tf_op jit(solution)/shard_map/all_to_all | solution.py:607
  202.5 1.7 spread_sum.1
  204.2 13.5 %all_to_all.26 = bf16[16,72,128]{2,1,0:T(8,128)(2,1)S(1)} all-to-all(bf16[16,72,128]{2,1,0:T(8,128)(2,1)} %spread_sum.1), channel_id=1, replica_groups=mesh['chip'=2,'core'=2,'dev'=8] {'chip','dev'}, dimensions={0} | all-to-all | bytes 589824 | tf_op jit(solution)/shard_map/all_to_all | solution.py:609
  218.4 0.6 broadcast_in_dim.24.moment_one
  219.0 0.6 broadcast_in_dim.25.moment_two
  219.6 0.8 copy.70.refs_12_
  220.4 0.8 copy.71.refs_14_
  221.1 0.6 pad_maximum_fusion.fixes
  221.7 0.7 copy-done.6
  222.4 6.3 %update.1 = (f32[1,1]{1,0:T(1,128)}, f32[2,128,256]{2,1,0:T(8,128)}, bf16[2,128,256]{2,1,0:T(8,128)(2,1)}, f32[2,128,128]{2,1,0:T(8,128)}, f32[2,256,256]{2,1,0:...) custom-call(s32[3]{0:T(128)} %pad_add_fusion.info, ...), custom_call_target="tpu_custom_call" | custom-call | flops 1073741824 | bytes 10485760 | tf_op jit(solution)/shard_map/update/pallas_call | solution.py:509
  228.8 2.0 copy.72
  230.7 1.8 copy.73
  232.5 2.0 copy.74
  234.5 1.3 reduce
  235.8 1.3 reduce.1
  237.1 1.3 reduce.2
  (28 shorter events, 0.1 us)
Async XLA Ops:
  28.5 3.0 %copy-start.2 = (s32[4224,15]{0,1:T(8,128)S(1)}, s32[4224,15]{0,1:T(8,128)}, u32[]{:S(2)}) copy-start(s32[4224,15]{0,1:T(8,128)} %param.34) | copy-start | bytes 760324
  28.5 53.0 %all-to-all-start.1 = ((bf16[32,256,128]{2,1,0:T(8,128)(2,1)}), bf16[32,256,128]{2,1,0:T(8,128)(2,1)S(1)}, u32[]{:S(2)}, u32[]{:S(2)}) async-start(bf16[32,256,128]{2,1,0:T(8,128)(2,1)} %bitcast.14), calls=%async_computation.1 | async-start | bytes 4194304 | tf_op jit(solution)/shard_map/all_to_all | solution.py:563
  31.4 2.2 copy-start.9
  31.4 3.0 %copy-start.10 = (s32[384,10]{0,1:T(8,128)S(1)}, s32[384,10]{0,1:T(8,128)}, u32[]{:S(2)}) copy-start(s32[384,10]{0,1:T(8,128)} %param.35) | copy-start | bytes 46084
  31.4 3.8 %copy-start.11 = (s32[64,5]{0,1:T(8,128)S(1)}, s32[64,5]{0,1:T(8,128)}, u32[]{:S(2)}) copy-start(s32[64,5]{0,1:T(8,128)} %param.33) | copy-start | bytes 3844
  31.4 4.5 %copy-start.12 = (s32[64,5]{0,1:T(8,128)S(1)}, s32[64,5]{0,1:T(8,128)}, u32[]{:S(2)}) copy-start(s32[64,5]{0,1:T(8,128)} %param.36) | copy-start | bytes 3844
  31.4 5.2 %copy-start.16 = (s32[64]{0:T(128)S(1)}, s32[64]{0:T(128)}, u32[]{:S(2)}) copy-start(s32[64]{0:T(128)} %param.37) | copy-start | bytes 772
  31.4 5.9 %copy-start.17 = (s32[64]{0:T(128)S(1)}, s32[64]{0:T(128)}, u32[]{:S(2)}) copy-start(s32[64]{0:T(128)} %param.38) | copy-start | bytes 772
  31.4 6.6 %copy-start.3 = (f32[2,256,172]{1,0,2:T(2,128)S(1)}, f32[2,256,172]{1,0,2:T(2,128)}, u32[]{:S(2)}) copy-start(f32[2,256,172]{1,0,2:T(2,128)} %param.41) | copy-start | bytes 1056772
  31.5 7.6 %copy-start.13 = (f32[684]{0:T(1024)S(1)}, f32[684]{0:T(1024)}, u32[]{:S(2)}) copy-start(f32[684]{0:T(1024)} %param.42) | copy-start | bytes 8212
  40.3 14.5 %copy-start.8 = (s32[4224,15]{0,1:T(8,128)S(1)}, s32[4224,15]{0,1:T(8,128)}, u32[]{:S(2)}) copy-start(s32[4224,15]{0,1:T(8,128)} %param.31) | copy-start | bytes 760324
  81.5 1.4 copy-start
  182.6 35.9 %copy-start.14 = (f32[684]{0:T(1024)S(1)}, f32[684]{0:T(1024)}, u32[]{:S(2)}) copy-start(f32[684]{0:T(1024)} %param.43) | copy-start | bytes 8212
  182.6 36.5 %copy-start.15 = (f32[684]{0:T(1024)S(1)}, f32[684]{0:T(1024)}, u32[]{:S(2)}) copy-start(f32[684]{0:T(1024)} %param.44) | copy-start | bytes 8212
  182.6 37.0 %copy-start.4 = (f32[2,172,172]{2,0,1:T(2,128)S(1)}, f32[2,172,172]{2,0,1:T(2,128)}, u32[]{:S(2)}) copy-start(f32[2,172,172]{2,0,1:T(2,128)} %param.51) | copy-start | bytes 710020
  182.6 37.8 %copy-start.5 = (f32[2,172,172]{2,0,1:T(2,128)S(1)}, f32[2,172,172]{2,0,1:T(2,128)}, u32[]{:S(2)}) copy-start(f32[2,172,172]{2,0,1:T(2,128)} %param.57) | copy-start | bytes 710020
  182.6 1.9 collective-permute-start
  184.4 0.7 copy-start.7
  217.7 4.0 %copy-start.1 = (bf16[16,72,128]{2,1,0:T(8,128)(2,1)}, bf16[16,72,128]{2,1,0:T(8,128)(2,1)S(1)}, u32[]{:S(2)}) copy-start(bf16[16,72,128]{2,1,0:T(8,128)(2,1)S(1)} %all_to_all.26) | copy-start | bytes 884740
  217.7 4.0 %collective-permute-start.1 = (bf16[1152,128]{1,0:T(8,128)(2,1)S(1)}, bf16[1152,128]{1,0:T(8,128)(2,1)S(1)}, u32[]{:S(2)}, u32[]{:S(2)}) collective-permute-start(bf16[1152,128]{1,0:T(8,128)(2,1)S(1)} %bitcast.16), channel_id=1, source_target_pairs={{0,8},{8,0},{1,9},{9,1},{2,10},{10,2},{3,11},{11,3},{4,12},{12,4},... | collective-permute-start | bytes 884744 | tf_op jit(solution)/shard_map/ppermute | solution.py:611
  221.7 0.7 copy-start.6

commit v2 on v1

v2 whole, which is shorter than its diff:
```python
import functools

import jax
import jax.numpy as jnp
from jax import lax
from jax.experimental import pallas as pl
from jax.experimental.pallas import tpu as pltpu
from jax.sharding import PartitionSpec as P

LANES = 128
SPAN = 256
PARTS = 2
AXES = ("chip", "core", "dev")
PEERS = ("chip", "dev")

smem = pl.BlockSpec(memory_space=pltpu.SMEM)
vmem = pl.BlockSpec(memory_space=pltpu.VMEM)
anywhere = pl.BlockSpec(memory_space=pl.ANY)


def up(value, unit):
    return -(-value // unit) * unit


def call(kernel, name, out_shape, in_specs, out_specs, scratch, flops, moved, room):
    return pl.pallas_call(
        kernel,
        name=name,
        out_shape=out_shape,
        in_specs=in_specs,
        out_specs=out_specs,
        scratch_shapes=scratch,
        compiler_params=pltpu.CompilerParams(vmem_limit_bytes=room),
        cost_estimate=pl.CostEstimate(flops=flops, transcendentals=0, bytes_accessed=moved),
    )


def dot(left, right):
    return jnp.dot(left, right, preferred_element_type=jnp.float32)


def dot_rows(left, right):
    return lax.dot_general(
        left, right, (((0,), (0,)), ((), ())), preferred_element_type=jnp.float32
    )


def dot_cols(left, right):
    return lax.dot_general(
        left, right, (((1,), (1,)), ((), ())), preferred_element_type=jnp.float32
    )


def halves(value):
    high = value.astype(jnp.bfloat16)
    return high, (value - high.astype(jnp.float32)).astype(jnp.bfloat16)


def grown(value, rows, columns):
    short = columns - value.shape[1]
    if short:
        value = jnp.concatenate([value, jnp.zeros((value.shape[0], short), value.dtype)], axis=1)
    short = rows - value.shape[0]
    if short:
        value = jnp.concatenate([value, jnp.zeros((short, columns), value.dtype)], axis=0)
    return value


def clipped_counts(valid):
    return jnp.maximum(jnp.sum(valid.astype(jnp.float32), axis=1, keepdims=True), 1.0)


def copy_rows(names, block, source, target):
    unroll = 16
    across = LANES // unroll

    def fetch(step, carry):
        row = block * (SPAN // LANES) + lax.div(step, across)
        column = lax.rem(step, across) * unroll
        for u in range(unroll):
            target[pl.ds(step * unroll + u, 1), :] = source[pl.ds(names[row, column + u], 1), :]
        return carry

    lax.fori_loop(0, SPAN // unroll, fetch, 0)


def pick_kernel(wanted, table, out, rows, *, first, part):
    unroll = min(32, part)
    steps = part // unroll

    def body(step, carry):
        device = lax.div(step, steps)
        column = first + lax.rem(step, steps) * unroll
        for u in range(unroll):
            rows[pl.ds(step * unroll + u, 1), :] = table[pl.ds(wanted[device, column + u], 1), :]
        return carry

    lax.fori_loop(0, wanted.shape[0] * steps, body, 0)
    out[...] = rows[...].astype(jnp.bfloat16)


def pick_rows(wanted, table, which):
    part, width = wanted.shape[1] // PARTS, table.shape[1]
    count = wanted.shape[0] * part
    return call(
        functools.partial(pick_kernel, first=which * part, part=part),
        "pick_rows",
        jax.ShapeDtypeStruct((count, width), jnp.bfloat16),
        [smem, vmem],
        vmem,
        [pltpu.VMEM((count, width), jnp.float32)],
        count * width,
        table.size * 4,
        20 << 20,
    )(wanted, table)


def reach_kernel(
    adjacent_three,
    valid_three,
    labelled,
    adjacent_two,
    valid_two,
    across_two,
    across_valid,
    names,
    places,
    count,
    left,
    right,
    *,
    rows_all,
    per,
):
    seeds, fan_three = adjacent_three.shape
    targets, fan_two = adjacent_two.shape
    low = jnp.bfloat16
    blocks = rows_all // LANES
    deep = names.shape[0]
    line = labelled[...].reshape(1, seeds)
    column = jnp.transpose(jnp.broadcast_to(line.astype(jnp.float32), (8, seeds)))[:, 0:1]
    live = (valid_three[...] > 0) & (column > 0.0)
    here = jnp.where(live, adjacent_three[...], -1)
    place = lax.broadcasted_iota(jnp.int32, (seeds, targets), 1)
    hit = jnp.zeros((seeds, targets), jnp.float32)
    for j in range(fan_three):
        hit = hit + jnp.where(here[:, j : j + 1] == place, 1.0, 0.0)
    need = jnp.max(hit, axis=0, keepdims=True) + jnp.concatenate(
        [line.astype(jnp.float32), jnp.zeros((1, targets - seeds), jnp.float32)], axis=1
    )

    level = lax.broadcasted_iota(jnp.int32, (deep, targets), 0)
    lane = lax.broadcasted_iota(jnp.int32, (targets, LANES), 1)
    flat = jnp.where((across_valid[...] > 0) & (need > 0.0), across_two[...], -1)
    tall = adjacent_two[...]
    for j in range(fan_two):
        left[0:deep, j * targets : (j + 1) * targets] = jnp.where(
            lax.shift_right_arithmetic(flat[j : j + 1, :], 7) == level, 1.0, 0.0
        ).astype(low)
        right[j * targets : (j + 1) * targets, :] = jnp.where(
            (tall[:, j : j + 1] & (LANES - 1)) == lane, 1.0, 0.0
        ).astype(low)
    used = dot(left[0:deep, 0 : fan_two * targets], right[0 : fan_two * targets, :])
    own = [need[:, k : k + LANES] for k in range(0, targets, LANES)]
    own = jnp.concatenate(
        own + [jnp.zeros((deep - len(own), LANES), jnp.float32)], axis=0
    )
    flag = jnp.where(used + own > 0.0, 1.0, 0.0)

    square_row = lax.broadcasted_iota(jnp.int32, (LANES, LANES), 0)
    square_col = lax.broadcasted_iota(jnp.int32, (LANES, LANES), 1)
    full = jnp.concatenate([flag, jnp.zeros((LANES - deep, LANES), jnp.float32)], axis=0)
    flag_low = full.astype(low)
    running = dot(flag_low, jnp.where(square_row <= square_col, 1.0, 0.0).astype(low))
    totals = dot(flag_low, jnp.ones((LANES, LANES), low)).astype(low)
    before = dot(jnp.where(square_row > square_col, 1.0, 0.0).astype(low), totals)
    order = (before + running - full).astype(jnp.int32)
    number = jnp.sum(flag).astype(jnp.int32)
    count[0] = number
    count[1] = lax.div(number + (SPAN - 1), SPAN)

    high = jnp.where(full > 0.0, lax.shift_right_arithmetic(order, 7), -1)
    rest = jnp.transpose((order & (LANES - 1)).astype(jnp.float32)).astype(jnp.int32)
    step = lax.broadcasted_iota(jnp.int32, (deep, LANES), 0)
    inner = lax.broadcasted_iota(jnp.int32, (deep, LANES), 1).astype(jnp.float32)
    for b in range(blocks):
        match = jnp.where(high[b : b + 1, :] == step, 1.0, 0.0)
        lanes = slice(b * LANES, (b + 1) * LANES)
        left[0:deep, lanes] = (match * inner).astype(low)
        left[deep : 2 * deep, lanes] = (match * float(b)).astype(low)
        right[lanes, :] = jnp.where(rest[:, b : b + 1] == square_col, 1.0, 0.0).astype(low)
    found = dot(left[:, 0:rows_all], right[0:rows_all, :]).astype(jnp.int32)
    where = step * LANES + lax.broadcasted_iota(jnp.int32, (deep, LANES), 1)
    name = found[deep:] * LANES + found[0:deep]
    names[...] = jnp.where(where < number, name, rows_all)
    name = jnp.minimum(jnp.where(where < number, name, 0), rows_all - 1)
    owner, slot = lax.div(name, per), lax.rem(name, per)
    part = per // PARTS
    owners = -(-rows_all // per)
    places[...] = lax.div(slot, part) * (owners * part) + owner * part + lax.rem(slot, part)


def reach(adjacent_three, valid_three, labelled, adjacent_two, valid_two, rows_all, per):
    targets, fan = adjacent_two.shape
    deep = up(up(rows_all, SPAN) // LANES, 16)
    area = max(fan * targets, rows_all)
    return call(
        functools.partial(reach_kernel, rows_all=rows_all, per=per),
        "reach",
        (
            jax.ShapeDtypeStruct((deep, LANES), jnp.int32),
            jax.ShapeDtypeStruct((deep, LANES), jnp.int32),
            jax.ShapeDtypeStruct((2,), jnp.int32),
        ),
        [vmem] * 7,
        (vmem, vmem, smem),
        [
            pltpu.VMEM((2 * deep, area), jnp.bfloat16),
            pltpu.VMEM((area, LANES), jnp.bfloat16),
        ],
        1 << 28,
        1 << 20,
        8 << 20,
    )(
        adjacent_three,
        valid_three,
        labelled,
        adjacent_two,
        valid_two,
        adjacent_two.T,
        valid_two.T,
    )


def tally_kernel(count, names, slots, *refs):
    outs = refs[:PARTS]
    rows, spread, code, buffer, sems = refs[PARTS:]
    low = jnp.bfloat16
    wide = outs[0].shape[1]
    high_all = PARTS * wide // SPAN
    fan = slots.shape[1]
    groups = SPAN // fan
    used = count[1]

    across = lax.broadcasted_iota(jnp.int32, (fan, SPAN), 1)
    down = lax.broadcasted_iota(jnp.int32, (fan, SPAN), 0)
    spread[...] = jnp.where(lax.div(across, fan) == down, 1.0, 0.0).astype(low)
    lane = lax.broadcasted_iota(jnp.int32, (fan, SPAN), 1)
    place = lax.broadcasted_iota(jnp.int32, (fan, SPAN), 0)

    def copies(block, slot):
        return [
            pltpu.make_async_copy(
                buffer.at[slot, :, pl.ds(part * wide, wide)],
                outs[part].at[pl.ds(pl.multiple_of(block * SPAN, SPAN), SPAN), :],
                sems.at[slot, part],
            )
            for part in range(PARTS)
        ]

    def body(block, carry):
        slot = lax.rem(block, 2)

        @pl.when(block >= 2)
        def _():
            for copy in copies(block - 2, slot):
                copy.wait()

        copy_rows(names, block, slots, rows)
        row = rows[...]
        high = lax.shift_right_arithmetic(row, 8).astype(jnp.float32).astype(low)
        lined = dot(high, spread[...])
        own = lax.rem(lax.broadcasted_iota(jnp.int32, (SPAN, SPAN), 0), fan) == lax.rem(
            lax.broadcasted_iota(jnp.int32, (SPAN, SPAN), 1), fan
        )
        lined = jnp.where(own, lined, 0.0).astype(low)
        member = (
            lax.div(lax.broadcasted_iota(jnp.int32, (groups, SPAN), 1), fan)
            == lax.broadcasted_iota(jnp.int32, (groups, SPAN), 0)
        )
        gathered = dot(jnp.where(member, 1.0, 0.0).astype(low), lined).astype(jnp.int32)
        code[...] = gathered * fan + lax.rem(
            lax.broadcasted_iota(jnp.int32, (groups, SPAN), 1), fan
        )

        def group(g, inner):
            first = pl.multiple_of(g * fan, fan)
            rest = rows[pl.ds(first, fan), :] & (SPAN - 1)
            columns = [
                jnp.where(jnp.broadcast_to(rest[:, j : j + 1], (fan, SPAN)) == lane, 1.0, 0.0)
                for j in range(fan)
            ]
            columns = jnp.concatenate(columns, axis=0).astype(low)
            line = jnp.broadcast_to(code[pl.ds(g, 1), :], (fan, SPAN))
            marks = [
                jnp.where(line == place + q * fan, 1.0, 0.0) for q in range(high_all)
            ]
            marks = jnp.concatenate(marks, axis=0).astype(low)
            result = dot(marks, columns).astype(low)
            for q in range(high_all):
                buffer[slot, pl.ds(first, fan), q * SPAN : (q + 1) * SPAN] = result[
                    q * fan : (q + 1) * fan
                ]
            return inner

        lax.fori_loop(0, groups, group, 0)
        for copy in copies(block, slot):
            copy.start()
        return carry

    lax.fori_loop(0, used, body, 0)

    @pl.when(used >= 2)
    def _():
        for copy in copies(used - 2, lax.rem(used - 2, 2)):
            copy.wait()

    @pl.when(used >= 1)
    def _():
        for copy in copies(used - 1, lax.rem(used - 1, 2)):
            copy.wait()


def tally(count, names, slots, padded, total):
    fan = slots.shape[1]
    wide = total // PARTS
    return call(
        tally_kernel,
        "tally",
        (jax.ShapeDtypeStruct((padded, wide), jnp.bfloat16),) * PARTS,
        [smem, smem, vmem],
        (anywhere,) * PARTS,
        [
            pltpu.VMEM((SPAN, fan), jnp.int32),
            pltpu.VMEM((fan, SPAN), jnp.bfloat16),
            pltpu.VMEM((SPAN // fan, SPAN), jnp.int32),
            pltpu.VMEM((2, SPAN, total), jnp.bfloat16),
            pltpu.SemaphoreType.DMA((2, PARTS)),
        ],
        1 << 32,
        32 << 20,
        20 << 20,
    )(count, names, slots)


def early_kernel(count, tallies, source, out, table, buffer, result, sems, out_sems):
    width = source.shape[1]
    used = count[1]
    table[:, 0:width] = source[...]
    table[:, width:] = jnp.ones((source.shape[0], width), jnp.bfloat16)

    def rows(block):
        return pl.ds(pl.multiple_of(block * SPAN, SPAN), SPAN)

    def load(block, slot):
        return pltpu.make_async_copy(tallies.at[rows(block), :], buffer.at[slot], sems.at[slot])

    def save(block, slot):
        return pltpu.make_async_copy(result.at[slot], out.at[rows(block), :], out_sems.at[slot])

    @pl.when(used > 0)
    def _():
        load(0, 0).start()

    def body(block, carry):
        slot = lax.rem(block, 2)
        load(block, slot).wait()

        @pl.when(block + 1 < used)
        def _():
            load(block + 1, 1 - slot).start()

        @pl.when(block >= 2)
        def _():
            save(block - 2, slot).wait()

        result[slot] = dot(buffer[slot], table[...])
        save(block, slot).start()
        return carry

    lax.fori_loop(0, used, body, 0)

    @pl.when(used >= 2)
    def _():
        save(used - 2, lax.rem(used - 2, 2)).wait()

    @pl.when(used >= 1)
    def _():
        save(used - 1, lax.rem(used - 1, 2)).wait()


def early_sums(count, tallies, source):
    padded, total = tallies.shape
    width = source.shape[1]
    return call(
        early_kernel,
        "early_sums",
        jax.ShapeDtypeStruct((padded, 2 * width), jnp.float32),
        [smem, anywhere, vmem],
        anywhere,
        [
            pltpu.VMEM((total, 2 * width), jnp.bfloat16),
            pltpu.VMEM((2, SPAN, total), jnp.bfloat16),
            pltpu.VMEM((2, SPAN, 2 * width), jnp.float32),
            pltpu.SemaphoreType.DMA((2,)),
            pltpu.SemaphoreType.DMA((2,)),
        ],
        1 << 32,
        16 << 20,
        16 << 20,
    )(count, tallies, source)


def link_kernel(count, names, adjacent, valid, out):
    targets, fan = adjacent.shape
    tile = 32
    blocks = count[1]

    def rows(step, carry):
        first = pl.multiple_of(step * tile, tile)
        here = jnp.where(
            valid[pl.ds(first, tile), :] > 0, adjacent[pl.ds(first, tile), :], -1
        )
        spread = [jnp.broadcast_to(here[:, j : j + 1], (tile, LANES)) for j in range(fan)]
        own = first + lax.broadcasted_iota(jnp.int32, (tile, LANES), 0)

        def columns(block, inner):
            for part in range(SPAN // LANES):
                name = jnp.broadcast_to(
                    names[pl.ds(block * (SPAN // LANES) + part, 1), :], (tile, LANES)
                )
                number = jnp.zeros((tile, LANES), jnp.float32)
                for j in range(fan):
                    number = number + jnp.where(spread[j] == name, 1.0, 0.0)
                lanes = pl.ds(part * LANES, LANES)
                out[block, pl.ds(first, tile), lanes] = number.astype(jnp.bfloat16)
                out[block, pl.ds(targets + first, tile), lanes] = jnp.where(
                    own == name, 1.0, 0.0
                ).astype(jnp.bfloat16)
            return inner

        return lax.fori_loop(0, blocks, columns, carry)

    lax.fori_loop(0, targets // tile, rows, 0)


def link_matrix(count, names, adjacent, valid, padded):
    blocks = padded // SPAN
    targets = adjacent.shape[0]
    return call(
        link_kernel,
        "link_matrix",
        jax.ShapeDtypeStruct((blocks, 2 * targets, SPAN), jnp.bfloat16),
        [smem, vmem, vmem, vmem],
        vmem,
        [],
        blocks * targets * SPAN * 30,
        blocks * targets * SPAN * 4,
        12 << 20,
    )(count, names, adjacent, valid)


def step_kernel(
    info,
    count,
    places,
    partial,
    tallies,
    links,
    *refs,
    classes,
    part,
):
    sources = refs[:PARTS]
    step_body(
        info, count, places, partial, tallies, links, sources, *refs[PARTS:],
        classes=classes, part=part,
    )


def step_body(
    info,
    count,
    places,
    partial,
    tallies,
    links,
    sources,
    valid_two,
    adjacent_three,
    valid_three,
    labels,
    labelled,
    weights_in,
    weights_mid,
    weights_out,
    biases_line,
    keep,
    send,
    slopes,
    packed,
    sums,
    weight_sums,
    mid_sums,
    out_sums,
    own_table,
    late_table,
    mixin,
    own_rows,
    joined,
    late,
    early,
    link,
    sems,
    link_sems,
    *,
    classes,
    part,
):
    blocks, both, _ = links.shape
    targets = both // 2
    hidden = weights_in.shape[2]
    seeds = labels.shape[0]
    biases = biases_line[...].reshape(1, biases_line.shape[0])
    label, marked = [
        jnp.transpose(
            jnp.broadcast_to(item[...].reshape(1, seeds).astype(jnp.float32), (8, seeds))
        )[:, 0:1]
        for item in (labels, labelled)
    ]
    wide = up(classes, LANES)
    core = info[0]
    used = count[1]
    low = jnp.bfloat16
    width = sources[0].shape[1]

    def load(block, slot):
        rows = pl.ds(pl.multiple_of(block * SPAN, SPAN), SPAN)
        return (
            pltpu.make_async_copy(tallies.at[rows, :], late.at[slot], sems.at[slot, 0]),
            pltpu.make_async_copy(partial.at[rows, :], early.at[slot], sems.at[slot, 1]),
        )

    def load_link(block):
        return pltpu.make_async_copy(links.at[block], link.at[block], link_sems.at[block])

    @pl.when(used > 0)
    def _():
        for copy in load(0, 0):
            copy.start()

    def start_link(block, carry):
        load_link(block).start()
        return carry

    lax.fori_loop(0, used, start_link, 0)
    late_table[:, 0:width] = sources[-1][...]
    late_table[:, width:] = jnp.ones((late_table.shape[0], width), low)
    held = own_table.shape[0] // PARTS
    for which in range(PARTS):
        own_table[which * held : (which + 1) * held, :] = sources[which][0:held, :].astype(
            jnp.float32
        )

    w_in = weights_in[...].astype(low).reshape(2 * weights_in.shape[1], hidden)
    bias_in = biases[:, 0:hidden]
    bias_mid = biases[:, hidden : 2 * hidden]
    bias_out = jnp.concatenate(
        [
            biases[:, 2 * hidden : 2 * hidden + classes],
            jnp.full((1, wide - classes), -1e30, jnp.float32),
        ],
        axis=1,
    )

    sums[...] = jnp.zeros_like(sums)

    def forward(block, carry):
        rows = pl.ds(pl.multiple_of(block * SPAN, SPAN), SPAN)
        slot = lax.rem(block, 2)
        for copy in load(block, slot):
            copy.wait()
        load_link(block).wait()

        @pl.when(block + 1 < used)
        def _():
            for copy in load(block + 1, 1 - slot):
                copy.start()

        copy_rows(places, block, own_table, own_rows)
        joined[...] = dot(late[slot], late_table[...]) + early[slot]
        mixin[rows, 0:width] = own_rows[...].astype(low)
        mixin[rows, width:] = (
            joined[:, 0:width] / jnp.maximum(joined[:, width:], 1.0)
        ).astype(low)
        z = dot(mixin[rows, :], w_in) + bias_in
        s = 1.0 / (1.0 + jnp.exp(-z))
        slopes[rows, :] = s * (1.0 + z * (1.0 - s))
        sums[...] += dot(link[block], (z * s).astype(low))
        return carry

    lax.fori_loop(0, used, forward, 0)
    total = sums[...]
    counts_two = clipped_counts(valid_two[...])
    mixed_one = (total[0:targets] / counts_two).astype(low)
    self_one = total[targets:].astype(low)
    w_mid = weights_mid[...].astype(low)
    both_one = jnp.concatenate([self_one, mixed_one], axis=1)
    z = dot(both_one, w_mid.reshape(2 * hidden, hidden)) + bias_mid
    s = 1.0 / (1.0 + jnp.exp(-z))
    slope_mid = s * (1.0 + z * (1.0 - s))
    hidden_two = (z * s).astype(low)

    here = jnp.where(valid_three[...] > 0, adjacent_three[...], -1)
    place = lax.broadcasted_iota(jnp.int32, (seeds, targets), 1)
    number = jnp.zeros((seeds, targets), jnp.float32)
    for j in range(here.shape[1]):
        number = number + jnp.where(here[:, j : j + 1] == place, 1.0, 0.0)
    number = number.astype(low)
    counts_three = clipped_counts(valid_three[...])
    mixed_two = (dot(number, hidden_two) / counts_three).astype(low)
    self_two = hidden_two[0:seeds]
    w_out = [
        jnp.concatenate(
            [weights_out[:, k, :], jnp.zeros((wide - classes, hidden), jnp.float32)], axis=0
        ).astype(low)
        for k in range(2)
    ]
    both_two = jnp.concatenate([self_two, mixed_two], axis=1)
    logits = dot_cols(both_two, jnp.concatenate(w_out, axis=1)) + bias_out
    top = jnp.max(logits, axis=1, keepdims=True)
    log_total = top + jnp.log(jnp.sum(jnp.exp(logits - top), axis=1, keepdims=True))
    onehot = jnp.where(
        label.astype(jnp.int32) == lax.broadcasted_iota(jnp.int32, (seeds, wide), 1), 1.0, 0.0
    )
    picked = jnp.sum(jnp.where(onehot > 0.0, logits, 0.0), axis=1, keepdims=True)
    loss = jnp.sum(marked * (log_total - picked), axis=0, keepdims=True)
    counted = jnp.sum(marked, axis=0, keepdims=True)
    grad_out = (marked * (jnp.exp(logits - log_total) - onehot)).astype(low)

    out_sums[...] = dot_rows(grad_out, both_two)
    bias_grad_out = jnp.sum(grad_out.astype(jnp.float32), axis=0, keepdims=True)
    to_self = dot(grad_out, w_out[0])
    spread = (dot(grad_out, w_out[1]) / counts_three).astype(low)
    sums[0:targets, :] = dot_rows(number, spread)
    sums[0:seeds, :] += to_self
    grad_mid = (sums[0:targets, :] * slope_mid).astype(low)

    mid_sums[...] = dot_rows(both_one, grad_mid)
    bias_grad_mid = jnp.sum(grad_mid.astype(jnp.float32), axis=0, keepdims=True)
    down = jnp.concatenate(
        [dot_cols(grad_mid, w_mid[1]) / counts_two, dot_cols(grad_mid, w_mid[0])], axis=0
    )
    spread = down.astype(low)

    weight_sums[...] = jnp.zeros_like(weight_sums)

    def backward(block, bias):
        rows = pl.ds(pl.multiple_of(block * SPAN, SPAN), SPAN)
        grad = (dot_rows(link[block], spread) * slopes[rows, :]).astype(low)
        weight_sums[...] += dot_rows(mixin[rows, :], grad)
        return bias + jnp.sum(grad.astype(jnp.float32), axis=0, keepdims=True)

    bias_grad_in = lax.fori_loop(0, used, backward, jnp.zeros((1, hidden), jnp.float32))

    row = 0
    for part in (weight_sums, mid_sums):
        for column in range(0, hidden, LANES):
            packed[row : row + part.shape[0], :] = part[:, column : column + LANES]
            row += part.shape[0]
    tall = up(classes, 16)
    for column in range(0, 2 * hidden, LANES):
        packed[row : row + tall, :] = out_sums[0:tall, column : column + LANES]
        row += tall
    packed[row:, :] = jnp.zeros((packed.shape[0] - row, LANES), jnp.float32)
    lane = lax.broadcasted_iota(jnp.int32, (1, LANES), 1)
    scalars = jnp.where(lane == 0, loss, 0.0) + jnp.where(lane == 1, counted, 0.0)
    extra = [
        item[:, column : column + LANES]
        for item in (bias_grad_in, bias_grad_mid, bias_grad_out)
        for column in range(0, hidden, LANES)
    ] + [scalars, jnp.zeros((1, LANES), jnp.float32)]
    extra = jnp.concatenate(extra, axis=0)
    high = extra.astype(low).astype(jnp.float32)
    packed[packed.shape[0] - 16 :, :] = jnp.concatenate([high, extra - high], axis=0)
    half = keep.shape[0]
    keep[...] = packed[pl.ds(pl.multiple_of(core * half, 16), half), :].astype(low)
    send[...] = packed[pl.ds(pl.multiple_of((1 - core) * half, 16), half), :].astype(low)


def run_step(info, count, places, partial, tallies, links, sources, rest, half, classes, part, owners):
    padded = partial.shape[0]
    blocks, both, _ = links.shape
    total, width = sources[0].shape
    hidden = rest[5].shape[2]
    wide = up(classes, LANES)
    return call(
        functools.partial(step_kernel, classes=classes, part=part),
        "step",
        (jax.ShapeDtypeStruct((half, LANES), jnp.bfloat16),) * 2,
        [smem] * 3 + [anywhere] * 3 + [vmem] * (PARTS + 9),
        (vmem, vmem),
        [
            pltpu.VMEM((padded, hidden), jnp.float32),
            pltpu.VMEM((2 * half, LANES), jnp.float32),
            pltpu.VMEM((both, hidden), jnp.float32),
            pltpu.VMEM((2 * width, hidden), jnp.float32),
            pltpu.VMEM((2 * hidden, hidden), jnp.float32),
            pltpu.VMEM((wide, 2 * hidden), jnp.float32),
            pltpu.VMEM((PARTS * owners * part, width), jnp.float32),
            pltpu.VMEM((total, 2 * width), jnp.bfloat16),
            pltpu.VMEM((padded, 2 * width), jnp.bfloat16),
            pltpu.VMEM((SPAN, width), jnp.float32),
            pltpu.VMEM((SPAN, 2 * width), jnp.float32),
            pltpu.VMEM((2, SPAN, total), jnp.bfloat16),
            pltpu.VMEM((2, SPAN, 2 * width), jnp.float32),
            pltpu.VMEM((blocks, both, SPAN), jnp.bfloat16),
            pltpu.SemaphoreType.DMA((2, 2)),
            pltpu.SemaphoreType.DMA((blocks,)),
        ],
        4 << 30,
        32 << 20,
        44 << 20,
    )(info, count, places, partial, tallies, links, *sources, *rest)


def refit(total, rows):
    extra = total[rows - 16 : rows - 8] + total[rows - 8 : rows]
    high = extra.astype(jnp.bfloat16).astype(jnp.float32)
    return jnp.concatenate([high, extra - high], axis=0)


def pair_kernel(info, mine, theirs, out):
    total = mine[...].astype(jnp.float32) + theirs[...].astype(jnp.float32)
    out[...] = total.astype(jnp.bfloat16)

    @pl.when(info[0] == 1)
    def _():
        rows = total.shape[0]
        out[rows - 16 :, :] = refit(total, rows).astype(jnp.bfloat16)


def pair_sum(info, mine, theirs):
    return call(
        pair_kernel,
        "pair_sum",
        jax.ShapeDtypeStruct(mine.shape, jnp.bfloat16),
        [smem, vmem, vmem],
        vmem,
        [],
        mine.size,
        mine.size * 6,
        6 << 20,
    )(info, mine, theirs)


def spread_kernel(info, pieces, out):
    total = pieces[0].astype(jnp.float32)
    for k in range(1, pieces.shape[0]):
        total = total + pieces[k].astype(jnp.float32)
    rows = total.shape[0]
    fitted = jnp.concatenate([total[0 : rows - 16], refit(total, rows)], axis=0)
    result = jnp.where(info[1] == 1, fitted, total).astype(jnp.bfloat16)
    for k in range(pieces.shape[0]):
        out[k] = result


def spread_sum(info, pieces):
    return call(
        spread_kernel,
        "spread_sum",
        jax.ShapeDtypeStruct(pieces.shape, jnp.bfloat16),
        [smem, vmem],
        vmem,
        [],
        pieces.size,
        pieces.size * 4,
        6 << 20,
    )(info, pieces)


def update_kernel(
    info, fixes, corners, mine, theirs, biases, moment_one, moment_two, *refs
):
    groups = [refs[3 * k : 3 * k + 3] for k in range(3)]
    loss_out = refs[9]
    outs = [refs[10 + 4 * k : 14 + 4 * k] for k in range(3)]
    bias_out, first_out, second_out = refs[22:25]
    packed = refs[25]
    low = jnp.bfloat16
    half = mine.shape[0]
    core = info[0]
    packed[pl.ds(pl.multiple_of(core * half, 16), half), :] = mine[...]
    packed[pl.ds(pl.multiple_of((1 - core) * half, 16), half), :] = theirs[...]
    last = packed.shape[0]
    extra = packed[last - 16 :, :].astype(jnp.float32)
    extra = extra[0:8] + extra[8:16]
    counted = extra[6:7, 1:2]
    inverse = 1.0 / counted
    loss_out[...] = extra[6:7, 0:1] / counted
    scale = 0.5 * inverse * inverse

    row = 0
    for group in range(3):
        master, left_root, right_root = groups[group]
        new_master, copy, new_left, new_right = outs[group]
        turned = group == 2
        depth, hidden = (master.shape[0], master.shape[2]) if turned else master.shape[1:]
        deep = up(depth, LANES)

        def take(ref, k, middle):
            return ref[:, k, :] if middle else ref[k]

        def put(ref, k, middle, value):
            if middle:
                ref[:, k, :] = value
            else:
                ref[k] = value

        grads = []
        if turned:
            tall = up(depth, 16)
            for k in range(2):
                parts = []
                for column in range(0, hidden, LANES):
                    parts.append(packed[row : row + tall, :])
                    row += tall
                grads.append(grown(jnp.concatenate(parts, axis=1), deep, hidden))
        else:
            parts = []
            for column in range(0, hidden, LANES):
                parts.append(packed[row : row + 2 * depth, :])
                row += 2 * depth
            whole = jnp.concatenate(parts, axis=1)
            grads = [whole[k * depth : (k + 1) * depth] for k in range(2)]

        for k in range(2):
            grad = grads[k]
            for side, new, size, product, middle in (
                (0, new_left, depth, dot_cols(grad, grad), turned),
                (1, new_right, hidden, dot_rows(grad, grad), False),
            ):
                corner = corners[group * 4 + side * 2 + k]
                eye = lax.broadcasted_iota(jnp.int32, (size, size), 0) == (
                    lax.broadcasted_iota(jnp.int32, (size, size), 1)
                )
                value = jnp.where(eye, 0.5 * corner, 0.0) + scale * product[0:size, 0:size]
                put(new, k, middle, value)
            root = jnp.concatenate(
                halves(grown(take(left_root, k, turned), deep, deep)), axis=1
            )
            middle_high, middle_rest = halves(dot(root, jnp.concatenate([grad, grad], axis=0)))
            root_high, root_rest = halves(right_root[k])
            way = dot(
                jnp.concatenate([middle_high, middle_high, middle_rest], axis=1),
                jnp.concatenate([root_high, root_rest, root_high], axis=0),
            )[0:depth]
            put(new_master, k, turned, take(master, k, turned) - inverse * way)
        copy[...] = new_master[...].astype(low)

    size = biases.shape[0]
    grad = jnp.concatenate([extra[k : k + 1, :] for k in range(6)], axis=1)[:, 0:size]
    grad = grad / counted

    def line(ref):
        return ref[...].reshape(1, size)

    first = 0.9 * line(moment_one) + 0.1 * grad
    second = 0.95 * line(moment_two) + 0.05 * grad * grad
    old = line(biases)
    fresh = old - 0.1 * (
        (first / fixes[0]) / (jnp.sqrt(second / fixes[1]) + 1e-08) + 0.01 * old
    )
    for ref, value in ((bias_out, fresh), (first_out, first), (second_out, second)):
        ref[...] = value[0]


def run_update(info, fixes, corners, mine, theirs, vectors, groups):
    outs = [jax.ShapeDtypeStruct((1, 1), jnp.float32)]
    flat = []
    for master, left_root, right_root in groups:
        flat += [master, left_root, right_root]
        outs += [
            jax.ShapeDtypeStruct(master.shape, jnp.float32),
            jax.ShapeDtypeStruct(master.shape, jnp.bfloat16),
            jax.ShapeDtypeStruct(left_root.shape, jnp.float32),
            jax.ShapeDtypeStruct(right_root.shape, jnp.float32),
        ]
    outs += [jax.ShapeDtypeStruct(vectors[0].shape, jnp.float32)] * 3
    return call(
        update_kernel,
        "update",
        tuple(outs),
        [smem] * 3 + [vmem] * (5 + len(flat)),
        (vmem,) * len(outs),
        [pltpu.VMEM((2 * mine.shape[0], LANES), jnp.bfloat16)],
        1 << 30,
        10 << 20,
        32 << 20,
    )(info, fixes, corners, mine, theirs, *vectors, *flat)


def body(
    features,
    requests,
    adjacent_one,
    adjacent_two,
    adjacent_three,
    valid_one,
    valid_two,
    valid_three,
    labels,
    labelled,
    weights_in,
    weights_mid,
    weights_out,
    biases,
    moment_one,
    moment_two,
    step_count,
    left_in,
    left_mid,
    left_out,
    right_in,
    right_mid,
    right_out,
    invleft_in,
    invleft_mid,
    invleft_out,
    invright_in,
    invright_mid,
    invright_out,
    *,
    peers,
):
    width = features.shape[1]
    devices, per = requests.shape
    part = per // PARTS
    total = devices * per
    targets, fan = adjacent_one.shape
    padded = up(targets, SPAN)
    owners = -(-targets // per)
    classes = weights_out.shape[2]
    hidden = weights_in.shape[2]
    core = lax.axis_index("core")
    own = lax.axis_index(PEERS)

    wanted = lax.all_to_all(requests, AXES, split_axis=0, concat_axis=0, tiled=True)
    sources = []
    for which in range(PARTS):
        found = pick_rows(wanted, features, which).reshape(devices, part, width)
        pulled = lax.all_to_all(found, AXES, split_axis=0, concat_axis=0, tiled=True)
        sources.append(pulled.reshape(devices * part, width))

    names, places, count = reach(
        adjacent_three, valid_three, labelled, adjacent_two, valid_two, targets, per
    )
    owner, slot = adjacent_one // per, adjacent_one % per
    slots = (slot // part) * (devices * part) + owner * part + slot % part
    slots = jnp.where(valid_one > 0, slots, -1)
    slots = jnp.pad(slots, ((0, 8), (0, 16 - fan)), constant_values=-1)
    tallies = tally(count, names, slots, padded, total)
    links = link_matrix(count, names, adjacent_two, valid_two, padded)
    partial = early_sums(count, tallies[0], sources[0])

    rows = (2 * width + 2 * weights_mid.shape[1]) * (hidden // LANES)
    rows += up(classes, 16) * (2 * hidden // LANES)
    each = up(-(-(rows + 16) // (2 * peers)), 8)
    half = each * peers
    info = jnp.stack([core, ((core == 1) & (own == peers - 1)).astype(jnp.int32)])
    info = info.astype(jnp.int32)
    turned_out = weights_out.transpose(2, 0, 1)
    keep, send = run_step(
        info,
        count,
        places,
        partial,
        tallies[1],
        links,
        sources,
        (
            valid_two,
            adjacent_three,
            valid_three,
            labels,
            labelled,
            weights_in,
            weights_mid,
            turned_out,
            biases,
        ),
        half,
        classes,
        part,
        owners,
    )
    swap = [(0, 1), (1, 0)]
    theirs = lax.ppermute(send, "core", swap)
    summed = pair_sum(info, keep, theirs).reshape(peers, each, LANES)
    pieces = lax.all_to_all(summed, PEERS, split_axis=0, concat_axis=0, tiled=True)
    shared = spread_sum(info, pieces)
    mine = lax.all_to_all(shared, PEERS, split_axis=0, concat_axis=0, tiled=True)
    mine = mine.reshape(half, LANES)
    theirs = lax.ppermute(mine, "core", swap)

    stepped = step_count.astype(jnp.float32)
    fixes = jnp.stack([1.0 - 0.9**stepped, 1.0 - 0.95**stepped])
    corners = jnp.concatenate(
        [
            item[:, 0, 0]
            for item in (left_in, right_in, left_mid, right_mid, right_out, left_out)
        ]
    )
    outs = run_update(
        info,
        fixes,
        corners,
        mine,
        theirs,
        (biases, moment_one, moment_two),
        (
            (weights_in, invleft_in, invright_in),
            (weights_mid, invleft_mid, invright_mid),
            (turned_out, invright_out.transpose(1, 0, 2), invleft_out),
        ),
    )
    first, second, third = (outs[1 + 4 * k : 5 + 4 * k] for k in range(3))
    third = (
        third[0].transpose(1, 2, 0),
        third[1].transpose(1, 2, 0),
        third[3],
        third[2].transpose(1, 0, 2),
    )
    return (
        (outs[0].reshape(()),)
        + tuple(group[which] for which in range(4) for group in (first, second, third))
        + tuple(outs[13:16])
    )


def solution(mesh):
    chips, dev = mesh.shape["hst"] // 2, mesh.shape["dev"]
    fine = jax.sharding.Mesh(mesh.devices.reshape(chips, 2, dev), AXES)
    split = P(AXES, None)
    line = P(AXES)
    whole = P()
    mapped = jax.shard_map(
        functools.partial(body, peers=chips * dev),
        mesh=fine,
        in_specs=(split,) * 8 + (line,) * 2 + (whole,) * 19,
        out_specs=(whole,) * 16,
        check_vma=False,
    )

    def run(*args):
        with jax.sharding.use_abstract_mesh(fine.abstract_mesh):
            return mapped(*args)

    return run
```

time: 239 us -> 211 us (0.88)
  Pallas kernels: 136 us -> 56.7 us
  blocking collectives: 43.3 us -> 85.2 us
  starting transfers between devices: 2.93 us -> 19.9 us
  waiting for transfers between devices: 27.7 us -> 16.4 us
  local copies, waits for them, and re-layouts: 20.3 us -> 24.1 us
    pallas_call x4 -> x7, Pallas kernels: 119 us -> 52.3 us  [the longest x2 26.1 us: pick_rows(): call(functools.partial(pick_kernel, first=which * part, part=part), 'pick...]
    all_to_all x1, blocking collectives: 15.5 us -> 70.9 us  [body(): lax.all_to_all(summed, PEERS, split_axis=0, concat_axis=0, tiled=True)]
    all_to_all x1 -> x0, blocking collectives: 13.5 us -> none  [body(): lax.all_to_all(shared, PEERS, split_axis=0, concat_axis=0, tiled=True)]
    pallas_call x1, Pallas kernels: 13.9 us -> 2.54 us  [link_matrix(): call(link_kernel, 'link_matrix', jax.ShapeDtypeStruct((blocks, 2 * target...]
    ppermute x1, starting transfers between devices: 0.07 us -> 10.9 us  [body(): theirs = lax.ppermute(send, 'core', swap)]
    all_to_all x1 -> x3, waiting for transfers between devices: 25.9 us -> 15.1 us  [the longest x1 7.63 us: body(): lax.all_to_all(shared, PEERS, split_axis=0, concat_axis=0, tiled=True)]
    all_to_all x1 -> x3, starting transfers between devices: 2.86 us -> 8.98 us  [the longest x2 5.44 us: body(): lax.all_to_all(found, AXES, split_axis=0, concat_axis=0, tiled=True)]
    select_n x0 -> x1, other arithmetic: none -> 5.38 us  [body(): slots = jnp.where(valid_one > 0, slots, -1)]
  transfers between devices with their start and end apart: 3 -> 5, of which waited for: 2 -> 3; matrix products, arithmetic and copies ran while one was open for 6% -> 6% of each run, Pallas kernels for 6% -> 14%
where the time goes in v2:
time: 211 us; the launch traced here: 210 us
  blocking collectives  85.2 us (40%)
  Pallas kernels  56.7 us (27%)
  local copies, waits for them, and re-layouts  24.1 us (11%)
  starting transfers between devices  19.9 us (9%)
  waiting for transfers between devices  16.4 us (8%)
  other arithmetic  5.57 us (3%)
    all_to_all x1, blocking collectives, body(): lax.all_to_all(summed, PEERS, split_axis=0, concat_axis=0, tiled=True)  70.9 us
    pallas_call x2, Pallas kernels, pick_rows(): call(functools.partial(pick_kernel, first=which * part, part=part), 'pick...  26.1 us
    unnamed x56, local copies, waits for them, and re-layouts  18.9 us
    all_to_all x1, blocking collectives, body(): lax.all_to_all(requests, AXES, split_axis=0, concat_axis=0, tiled=True)  14.3 us
    ppermute x1, starting transfers between devices, body(): theirs = lax.ppermute(send, 'core', swap)  10.9 us
    pallas_call x1, Pallas kernels, tally(): call(tally_kernel, 'tally', (jax.ShapeDtypeStruct((padded, wide), jnp.bfl...  9.04 us
    all_to_all x1, waiting for transfers between devices, body(): lax.all_to_all(shared, PEERS, split_axis=0, concat_axis=0, tiled=True)  7.63 us
    all_to_all x2, waiting for transfers between devices, body(): lax.all_to_all(found, AXES, split_axis=0, concat_axis=0, tiled=True)  7.52 us
  transfers between devices with their start and end apart: 5, of which 3 were waited for; matrix products, arithmetic and copies ran while one was open for 6% of the time, Pallas kernels for 14%

profile of v2, /device:TPU:0, one launch (start us, length us, event | category | flops | bytes accessed | tf_op | source)
XLA Modules:
  0.0 209.7 jit_solution(7666700245256318415)
XLA Ops:
  0.6 0.8 all_to_all.19
  1.4 14.3 %all_to_all.31 = s32[32,1,256]{2,1,0:T(1,128)S(1)} all-to-all(s32[32,1,256]{2,1,0:T(1,128)S(1)} %all_to_all.19), channel_id=1, replica_groups=mesh['chip'=2,'core'=2,'dev'=8] {'chip','core','dev'}, dimensions={0} | all-to-all | bytes 65536 | tf_op jit(solution)/shard_map/all_to_all | solution.py:948
  15.7 3.4 %copy-done = f32[16384,128]{1,0:T(8,128)S(1)} copy-done((f32[16384,128]{1,0:T(8,128)S(1)}, f32[16384,128]{1,0:T(8,128)}, u32[]{:S(2)}) %copy-start) | copy-done | bytes 8388632
  19.1 13.0 %pick_rows.2 = bf16[4096,128]{1,0:T(8,128)(2,1)} custom-call(s32[32,256]{1,0:T(8,128)S(1)} %bitcast.30, f32[16384,128]{1,0:T(8,128)S(1)} %copy-done), custom_call_target="tpu_custom_call" | custom-call | flops 524288 | bytes 8388608 | tf_op jit(solution)/shard_map/pick_rows/pallas_call | solution.py:105
  32.1 0.0 copy-start.22
  32.1 2.8 %all-to-all-start.1 = ((bf16[32,128,128]{2,1,0:T(8,128)(2,1)}), bf16[32,128,128]{2,1,0:T(8,128)(2,1)S(1)}, u32[]{:S(2)}, u32[]{:S(2)}) async-start(bf16[32,128,128]{2,1,0:T(8,128)(2,1)} %bitcast.6), calls=%async_computation.1 | async-start | bytes 2097152 | tf_op jit(solution)/shard_map/all_to_all | solution.py:952
  35.0 0.1 copy.78.valid_two.valid.refs_2_
  35.1 0.1 copy.77.adjacent_two.adjacent
  35.3 0.1 copy.75.adjacent_three.refs_3_
  35.4 0.1 copy.76.valid_three.refs_4_
  35.5 2.1 copy.80
  37.6 1.0 copy.84
  38.5 0.0 copy-start.1
  38.5 3.4 %copy-done.1 = f32[16384,128]{1,0:T(8,128)S(1)} copy-done((f32[16384,128]{1,0:T(8,128)S(1)}, f32[16384,128]{1,0:T(8,128)}, u32[]{:S(2)}) %copy-start.1) | copy-done | bytes 8388632
  41.9 13.1 %pick_rows.3 = bf16[4096,128]{1,0:T(8,128)(2,1)} custom-call(s32[32,256]{1,0:T(8,128)S(1)} %bitcast.31, f32[16384,128]{1,0:T(8,128)S(1)} %copy-done.1), custom_call_target="tpu_custom_call" | custom-call | flops 524288 | bytes 8388608 | tf_op jit(solution)/shard_map/pick_rows/pallas_call | solution.py:105
  55.0 7.5 %all-to-all-done.1 = bf16[32,128,128]{2,1,0:T(8,128)(2,1)S(1)} async-done(((bf16[32,128,128]{2,1,0:T(8,128)(2,1)}), bf16[32,128,128]{2,1,0:T(8,128)(2,1)S(1)}, u32[]{:S(2)}, u32[]{:S(2)}) %all-to-all-start.1) | async-done | bytes 1048608 | tf_op jit(solution)/shard_map/all_to_all | solution.py:952
  62.5 2.6 %all-to-all-start.2 = ((bf16[32,128,128]{2,1,0:T(8,128)(2,1)}), bf16[32,128,128]{2,1,0:T(8,128)(2,1)S(1)}, u32[]{:S(2)}, u32[]{:S(2)}) async-start(bf16[32,128,128]{2,1,0:T(8,128)(2,1)} %bitcast.8), calls=%async_computation.2 | async-start | bytes 2097152 | tf_op jit(solution)/shard_map/all_to_all | solution.py:952
  65.2 5.4 %fusion.3 = s32[4224,15]{1,0:T(8,128)S(1)} fusion(pred[4224,15]{1,0:T(8,128)(4,1)S(1)} %copy.84, s32[4224,15]{1,0:T(8,128)} %copy.80), kind=kLoop, calls=%fused_computation.13 | loop fusion | flops 2724480 | bytes 570240 | tf_op jit(solution)/shard_map/jit(_where)/select_n | solution.py:960
  70.6 0.1 pad.4.slots
  70.7 0.5 copy-done.19
  71.2 2.6 %reach.1 = (s32[48,128]{1,0:T(8,128)S(1)}, s32[48,128]{1,0:T(8,128)S(1)}, s32[2]{0:T(128)S(1)}) custom-call(s32[64,5]{1,0:T(8,128)S(1)} %copy.75.adjacent_three.refs_3_, s32[64,5]{1,0:T(8,128)S(1)} %copy.76.valid_three.refs_4_, s32[64]{0:T(128)S(1)} %copy-done.19, s32[384,10]{1,0:T(8,128)S(1)} %copy.77.adjacent_two.adjacent, ...), custom_call_target="tpu_custom_call" | custom-call | flops 268435456 | bytes 1048576 | tf_op jit(solution)/shard_map/reach/pallas_call | solution.py:207
  73.8 2.5 %link_matrix.1.links = bf16[17,768,256]{2,1,0:T(8,128)(2,1)S(1)} custom-call(s32[2]{0:T(128)S(1)} %get-tuple-element.39.count, s32[48,128]{1,0:T(8,128)S(1)} %get-tuple-element.41.names, s32[384,10]{1,0:T(8,128)S(1)} %copy.77.adjacent_two.adjacent, s32[384,10]{1,0:T(8,128)S(1)} %copy.78.valid_two.valid.refs_2_), custom_call_target="tpu_custom_call" | custom-call | flops 50135040 | bytes 6684672 | tf_op jit(solution)/shard_map/link_matrix/pallas_call | solution.py:450
  76.3 2.7 %copy-done.2 = bf16[17,768,256]{2,1,0:T(8,128)(2,1)} copy-done((bf16[17,768,256]{2,1,0:T(8,128)(2,1)}, bf16[17,768,256]{2,1,0:T(8,128)(2,1)S(1)}, u32[]{:S(2)}) %copy-start.2) | copy-done | bytes 6684696
  79.1 0.1 pad_add_fusion.info
  79.1 9.0 %tally.1 = (bf16[4352,4096]{1,0:T(8,128)(2,1)}, bf16[4352,4096]{1,0:T(8,128)(2,1)}) custom-call(s32[2]{0:T(128)S(1)} %get-tuple-element.39.count, s32[48,128]{1,0:T(8,128)S(1)} %get-tuple-element.41.names, s32[4232,16]{1,0:T(8,128)S(1)} %pad.4.slots), custom_call_target="tpu_custom_call" | custom-call | flops 4294967296 | bytes 33554432 | tf_op jit(solution)/shard_map/tally/pallas_call | solution.py:327
  88.2 0.0 copy-start.7
  88.2 0.0 copy-start.16
  88.2 3.1 %early_sums.1.partial = f32[4352,256]{1,0:T(8,128)S(1)} custom-call(s32[2]{0:T(128)S(1)} %get-tuple-element.39.count, bf16[4352,4096]{1,0:T(8,128)(2,1)} %get-tuple-element.42.tallies, bf16[4096,128]{1,0:T(8,128)(2,1)S(1)} %bitcast.21), custom_call_target="tpu_custom_call" | custom-call | flops 4294967296 | bytes 16777216 | tf_op jit(solution)/shard_map/early_sums/pallas_call | solution.py:395
  91.3 2.0 copy-done.3
  93.4 2.3 %copy-done.4 = f32[4352,256]{1,0:T(8,128)S(1)} copy-done((f32[4352,256]{1,0:T(8,128)S(1)}, f32[4352,256]{1,0:T(8,128)}, u32[]{:S(2)}) %copy-start.4) | copy-done | bytes 4456472
  95.7 7.1 %step.1 = (bf16[1152,128]{1,0:T(8,128)(2,1)S(1)}, bf16[1152,128]{1,0:T(8,128)(2,1)S(1)}) custom-call(s32[2]{0:T(128)S(1)} %pad_add_fusion.info, s32[2]{0:T(128)S(1)} %get-tuple-element.39.count, s32[48,128]{1,0:T(8,128)S(1)} %get-tuple-element.40.places, f32[4352,256]{1,0:T(8,128)S(1)} %copy-done.4, bf16[4352,4096]{1,0:T(8,128)(2,1)} %get-tuple-element.43.tallies, ...), custom_call_target="tpu_custom_call" | custom-call | flops 4294967296 | bytes 33554432 | tf_op jit(solution)/shard_map/step/pallas_call | solution.py:697
  102.8 0.0 copy-start.9
  102.8 10.9 %collective-permute-start = (bf16[1152,128]{1,0:T(8,128)(2,1)S(1)}, bf16[1152,128]{1,0:T(8,128)(2,1)S(1)}, u32[]{:S(2)}, u32[]{:S(2)}) collective-permute-start(bf16[1152,128]{1,0:T(8,128)(2,1)S(1)} %get-tuple-element.45), channel_id=1, source_target_pairs={{0,8},{8,0},{1,9},{9,1},{2,10},{10,2},{3,11},{11,3},{4,12},{12,4},... | collective-permute-start | bytes 884744 | tf_op jit(solution)/shard_map/ppermute | solution.py:998
  113.8 1.2 collective-permute-done.theirs
  115.0 0.6 pair_sum.1
  115.6 70.9 %all_to_all.32.pieces = bf16[16,72,128]{2,1,0:T(8,128)(2,1)S(1)} all-to-all(bf16[16,72,128]{2,1,0:T(8,128)(2,1)S(1)} %bitcast.28), channel_id=1, replica_groups=mesh['chip'=2,'core'=2,'dev'=8] {'chip','dev'}, dimensions={0} | all-to-all | bytes 589824 | tf_op jit(solution)/shard_map/all_to_all | solution.py:1000
  186.5 1.3 spread_sum.1
  187.8 3.5 %all-to-all-start.4 = ((bf16[16,72,128]{2,1,0:T(8,128)(2,1)}), bf16[16,72,128]{2,1,0:T(8,128)(2,1)S(1)}, u32[]{:S(2)}, u32[]{:S(2)}) async-start(bf16[16,72,128]{2,1,0:T(8,128)(2,1)} %spread_sum.1), calls=%async_computation.4 | async-start | bytes 589824 | tf_op jit(solution)/shard_map/all_to_all | solution.py:1002
  192.1 0.8 slice_reduce_fusion.5
  192.9 0.8 slice_reduce_fusion
  193.7 7.6 %all-to-all-done.4 = bf16[16,72,128]{2,1,0:T(8,128)(2,1)S(1)} async-done(((bf16[16,72,128]{2,1,0:T(8,128)(2,1)}), bf16[16,72,128]{2,1,0:T(8,128)(2,1)S(1)}, u32[]{:S(2)}, u32[]{:S(2)}) %all-to-all-start.4) | async-done | bytes 294944 | tf_op jit(solution)/shard_map/all_to_all | solution.py:1002
  201.3 0.8 slice_reduce_fusion.1
  202.1 0.8 slice_reduce_fusion.3
  202.9 0.1 concatenate.3.corners
  203.0 0.1 pad_maximum_fusion.fixes
  203.1 1.0 copy-done.11
  204.2 1.0 copy-done.12
  205.2 4.4 %update.1 = (f32[1,1]{1,0:T(1,128)}, f32[2,128,256]{2,1,0:T(8,128)}, bf16[2,128,256]{2,1,0:T(8,128)(2,1)}, f32[2,128,128]{2,1,0:T(8,128)}, f32[2,256,256]{2,1,0:...) custom-call(s32[2]{0:T(128)S(1)} %pad_add_fusion.info, ...), custom_call_target="tpu_custom_call" | custom-call | flops 1073741824 | bytes 10485760 | tf_op jit(solution)/shard_map/update/pallas_call | solution.py:890
  (42 shorter events, 0.1 us)
Async XLA Ops:
  15.7 3.4 %copy-start = (f32[16384,128]{1,0:T(8,128)S(1)}, f32[16384,128]{1,0:T(8,128)}, u32[]{:S(2)}) copy-start(f32[16384,128]{1,0:T(8,128)} %table.3) | copy-start | bytes 25165828
  19.1 15.8 %copy-start.15 = (s32[384,10]{0,1:T(8,128)S(1)}, s32[384,10]{0,1:T(8,128)}, u32[]{:S(2)}) copy-start(s32[384,10]{0,1:T(8,128)} %param.35) | copy-start | bytes 46084
  32.1 3.0 %copy-start.14 = (s32[384,10]{0,1:T(8,128)S(1)}, s32[384,10]{0,1:T(8,128)}, u32[]{:S(2)}) copy-start(s32[384,10]{0,1:T(8,128)} %param.32) | copy-start | bytes 46084
  32.1 3.1 %copy-start.23 = (s32[64,5]{0,1:T(8,128)S(1)}, s32[64,5]{0,1:T(8,128)}, u32[]{:S(2)}) copy-start(s32[64,5]{0,1:T(8,128)} %param.33) | copy-start | bytes 3844
  32.1 3.2 %copy-start.24 = (s32[64,5]{0,1:T(8,128)S(1)}, s32[64,5]{0,1:T(8,128)}, u32[]{:S(2)}) copy-start(s32[64,5]{0,1:T(8,128)} %param.36) | copy-start | bytes 3844
  32.1 3.3 %copy-start.21 = (s32[4224,15]{0,1:T(8,128)S(1)}, s32[4224,15]{0,1:T(8,128)}, u32[]{:S(2)}) copy-start(s32[4224,15]{0,1:T(8,128)} %param.31) | copy-start | bytes 760324
  32.1 5.4 %copy-start.22 = (s32[4224,15]{0,1:T(8,128)S(1)}, s32[4224,15]{0,1:T(8,128)}, u32[]{:S(2)}) copy-start(s32[4224,15]{0,1:T(8,128)} %param.34) | copy-start | bytes 760324
  32.1 30.4 %all-to-all-start.1 = ((bf16[32,128,128]{2,1,0:T(8,128)(2,1)}), bf16[32,128,128]{2,1,0:T(8,128)(2,1)S(1)}, u32[]{:S(2)}, u32[]{:S(2)}) async-start(bf16[32,128,128]{2,1,0:T(8,128)(2,1)} %bitcast.6), calls=%async_computation.1 | async-start | bytes 2097152 | tf_op jit(solution)/shard_map/all_to_all | solution.py:952
  38.5 3.4 %copy-start.1 = (f32[16384,128]{1,0:T(8,128)S(1)}, f32[16384,128]{1,0:T(8,128)}, u32[]{:S(2)}) copy-start(f32[16384,128]{1,0:T(8,128)} %table.3) | copy-start | bytes 25165828
  62.5 30.9 %all-to-all-start.2 = ((bf16[32,128,128]{2,1,0:T(8,128)(2,1)}), bf16[32,128,128]{2,1,0:T(8,128)(2,1)S(1)}, u32[]{:S(2)}, u32[]{:S(2)}) async-start(bf16[32,128,128]{2,1,0:T(8,128)(2,1)} %bitcast.8), calls=%async_computation.2 | async-start | bytes 2097152 | tf_op jit(solution)/shard_map/all_to_all | solution.py:952
  70.6 0.7 copy-start.19
  76.3 2.7 %copy-start.2 = (bf16[17,768,256]{2,1,0:T(8,128)(2,1)}, bf16[17,768,256]{2,1,0:T(8,128)(2,1)S(1)}, u32[]{:S(2)}) copy-start(bf16[17,768,256]{2,1,0:T(8,128)(2,1)S(1)} %link_matrix.1.links) | copy-start | bytes 20054020
  88.2 5.2 %copy-start.5 = (f32[2,256,256]{2,1,0:T(8,128)S(1)}, f32[2,256,256]{2,1,0:T(8,128)}, u32[]{:S(2)}) copy-start(f32[2,256,256]{2,1,0:T(8,128)} %refs_3_.2) | copy-start | bytes 1572868
  88.2 5.2 %copy-start.6 = (f32[2,256,172]{1,0,2:T(2,128)S(1)}, f32[2,256,172]{1,0,2:T(2,128)}, u32[]{:S(2)}) copy-start(f32[2,256,172]{1,0,2:T(2,128)} %param.41) | copy-start | bytes 1056772
  88.2 5.2 %copy-start.7 = (f32[2,128,256]{2,1,0:T(8,128)S(1)}, f32[2,128,256]{2,1,0:T(8,128)}, u32[]{:S(2)}) copy-start(f32[2,128,256]{2,1,0:T(8,128)} %refs_0_.1) | copy-start | bytes 786436
  88.2 5.2 %copy-start.16 = (f32[684]{0:T(1024)S(1)}, f32[684]{0:T(1024)}, u32[]{:S(2)}) copy-start(f32[684]{0:T(1024)} %biases.1) | copy-start | bytes 8212
  88.2 5.2 %copy-start.20 = (s32[64]{0:T(128)S(1)}, s32[64]{0:T(128)}, u32[]{:S(2)}) copy-start(s32[64]{0:T(128)} %refs_5_.2) | copy-start | bytes 772
  91.3 2.0 copy-start.3
  93.4 2.3 %copy-start.4 = (f32[4352,256]{1,0:T(8,128)S(1)}, f32[4352,256]{1,0:T(8,128)}, u32[]{:S(2)}) copy-start(f32[4352,256]{1,0:T(8,128)} %copy-done.3) | copy-start | bytes 13369348
  102.8 100.3 %copy-start.8 = (f32[2,256,256]{2,1,0:T(8,128)S(1)}, f32[2,256,256]{2,1,0:T(8,128)}, u32[]{:S(2)}) copy-start(f32[2,256,256]{2,1,0:T(8,128)} %refs_2_.2) | copy-start | bytes 1572868
  102.8 100.3 %copy-start.9 = (f32[2,256,256]{2,1,0:T(8,128)S(1)}, f32[2,256,256]{2,1,0:T(8,128)}, u32[]{:S(2)}) copy-start(f32[2,256,256]{2,1,0:T(8,128)} %refs_4_.2) | copy-start | bytes 1572868
  102.8 100.3 %copy-start.10 = (f32[2,256,256]{2,1,0:T(8,128)S(1)}, f32[2,256,256]{2,1,0:T(8,128)}, u32[]{:S(2)}) copy-start(f32[2,256,256]{2,1,0:T(8,128)} %refs_5_.3) | copy-start | bytes 1572868
  102.8 100.3 %copy-start.13 = (f32[2,128,128]{2,1,0:T(8,128)S(1)}, f32[2,128,128]{2,1,0:T(8,128)}, u32[]{:S(2)}) copy-start(f32[2,128,128]{2,1,0:T(8,128)} %refs_1_.1) | copy-start | bytes 393220
  102.8 100.3 %copy-start.17 = (f32[684]{0:T(1024)S(1)}, f32[684]{0:T(1024)}, u32[]{:S(2)}) copy-start(f32[684]{0:T(1024)} %moment_one.1) | copy-start | bytes 8212
  102.8 100.3 %copy-start.18 = (f32[684]{0:T(1024)S(1)}, f32[684]{0:T(1024)}, u32[]{:S(2)}) copy-start(f32[684]{0:T(1024)} %moment_two.1) | copy-start | bytes 8212
  102.8 12.1 %collective-permute-start = (bf16[1152,128]{1,0:T(8,128)(2,1)S(1)}, bf16[1152,128]{1,0:T(8,128)(2,1)S(1)}, u32[]{:S(2)}, u32[]{:S(2)}) collective-permute-start(bf16[1152,128]{1,0:T(8,128)(2,1)S(1)} %get-tuple-element.45), channel_id=1, source_target_pairs={{0,8},{8,0},{1,9},{9,1},{2,10},{10,2},{3,11},{11,3},{4,12},{12,4},... | collective-permute-start | bytes 884744 | tf_op jit(solution)/shard_map/ppermute | solution.py:998
  187.8 13.5 %all-to-all-start.4 = ((bf16[16,72,128]{2,1,0:T(8,128)(2,1)}), bf16[16,72,128]{2,1,0:T(8,128)(2,1)S(1)}, u32[]{:S(2)}, u32[]{:S(2)}) async-start(bf16[16,72,128]{2,1,0:T(8,128)(2,1)} %spread_sum.1), calls=%async_computation.4 | async-start | bytes 589824 | tf_op jit(solution)/shard_map/all_to_all | solution.py:1002
  201.3 1.8 collective-permute-start.1
  203.1 1.0 copy-start.11
  204.2 1.0 copy-start.12

commit v3 on v2

--- a/solution.py
+++ b/solution.py
@@ -15,7 +15,7 @@
 
 smem = pl.BlockSpec(memory_space=pltpu.SMEM)
 vmem = pl.BlockSpec(memory_space=pltpu.VMEM)
-anywhere = pl.BlockSpec(memory_space=pl.ANY)
+anywhere = pl.BlockSpec(memory_space=pltpu.HBM)
 
 
 def up(value, unit):
@@ -71,39 +71,41 @@
 
 
 def copy_rows(names, block, source, target):
-    unroll = 16
-    across = LANES // unroll
+    unroll = 64
+    base = block * SPAN
 
     def fetch(step, carry):
-        row = block * (SPAN // LANES) + lax.div(step, across)
-        column = lax.rem(step, across) * unroll
         for u in range(unroll):
-            target[pl.ds(step * unroll + u, 1), :] = source[pl.ds(names[row, column + u], 1), :]
+            at = step * unroll + u
+            target[pl.ds(at, 1), :] = source[pl.ds(names[base + at], 1), :]
         return carry
 
     lax.fori_loop(0, SPAN // unroll, fetch, 0)
 
 
-def pick_kernel(wanted, table, out, rows, *, first, part):
-    unroll = min(32, part)
-    steps = part // unroll
-
-    def body(step, carry):
-        device = lax.div(step, steps)
-        column = first + lax.rem(step, steps) * unroll
-        for u in range(unroll):
-            rows[pl.ds(step * unroll + u, 1), :] = table[pl.ds(wanted[device, column + u], 1), :]
+def cuts(per):
+    return (0, per - per // 4), (per - per // 4, per)
+
+
+def pick_kernel(wanted, table, out, rows, *, first, last, per):
+    part = last - first
+
+    def body(device, carry):
+        for u in range(part):
+            name = wanted[device * per + (first + u)]
+            rows[pl.ds(device * part + u, 1), :] = table[pl.ds(name, 1), :]
         return carry
 
-    lax.fori_loop(0, wanted.shape[0] * steps, body, 0)
+    lax.fori_loop(0, out.shape[0] // part, body, 0)
     out[...] = rows[...].astype(jnp.bfloat16)
 
 
-def pick_rows(wanted, table, which):
-    part, width = wanted.shape[1] // PARTS, table.shape[1]
-    count = wanted.shape[0] * part
+def pick_rows(wanted, table, per, ends):
+    first, last = ends
+    width = table.shape[1]
+    count = wanted.shape[0] // per * (last - first)
     return call(
-        functools.partial(pick_kernel, first=which * part, part=part),
+        functools.partial(pick_kernel, first=first, last=last, per=per),
         "pick_rows",
         jax.ShapeDtypeStruct((count, width), jnp.bfloat16),
         [smem, vmem],
@@ -115,16 +117,26 @@
     )(wanted, table)
 
 
+def stood(flat, unit):
+    size = flat.shape[1]
+    flat = jnp.concatenate(
+        [flat, jnp.full((unit - flat.shape[0], size), -1, jnp.int32)], axis=0
+    ).astype(jnp.float32)
+    step = min(LANES, size)
+    parts = [jnp.transpose(flat[:, k : k + step]) for k in range(0, size, step)]
+    return jnp.concatenate(parts, axis=0).astype(jnp.int32)
+
+
 def reach_kernel(
     adjacent_three,
     valid_three,
     labelled,
     adjacent_two,
     valid_two,
-    across_two,
-    across_valid,
     names,
     places,
+    near_two,
+    near_three,
     count,
     left,
     right,
@@ -132,15 +144,16 @@
     rows_all,
     per,
 ):
-    seeds, fan_three = adjacent_three.shape
-    targets, fan_two = adjacent_two.shape
+    fan_three, seeds = adjacent_three.shape
+    fan_two, targets = adjacent_two.shape
     low = jnp.bfloat16
     blocks = rows_all // LANES
     deep = names.shape[0]
     line = labelled[...].reshape(1, seeds)
     column = jnp.transpose(jnp.broadcast_to(line.astype(jnp.float32), (8, seeds)))[:, 0:1]
-    live = (valid_three[...] > 0) & (column > 0.0)
-    here = jnp.where(live, adjacent_three[...], -1)
+    near = stood(jnp.where(valid_three[...] > 0, adjacent_three[...], -1), near_three.shape[1])
+    near_three[...] = near
+    here = jnp.where(column > 0.0, near, -1)
     place = lax.broadcasted_iota(jnp.int32, (seeds, targets), 1)
     hit = jnp.zeros((seeds, targets), jnp.float32)
     for j in range(fan_three):
@@ -151,8 +164,10 @@
 
     level = lax.broadcasted_iota(jnp.int32, (deep, targets), 0)
     lane = lax.broadcasted_iota(jnp.int32, (targets, LANES), 1)
-    flat = jnp.where((across_valid[...] > 0) & (need > 0.0), across_two[...], -1)
-    tall = adjacent_two[...]
+    flat = jnp.where(valid_two[...] > 0, adjacent_two[...], -1)
+    tall = stood(flat, near_two.shape[1])
+    near_two[...] = tall
+    flat = jnp.where(need > 0.0, flat, -1)
     for j in range(fan_two):
         left[0:deep, j * targets : (j + 1) * targets] = jnp.where(
             lax.shift_right_arithmetic(flat[j : j + 1, :], 7) == level, 1.0, 0.0
@@ -194,14 +209,18 @@
     name = found[deep:] * LANES + found[0:deep]
     names[...] = jnp.where(where < number, name, rows_all)
     name = jnp.minimum(jnp.where(where < number, name, 0), rows_all - 1)
-    owner, slot = lax.div(name, per), lax.rem(name, per)
-    part = per // PARTS
     owners = -(-rows_all // per)
-    places[...] = lax.div(slot, part) * (owners * part) + owner * part + lax.rem(slot, part)
+    owner = lax.shift_right_logical(name, per.bit_length() - 1)
+    slot = name & (per - 1)
+    early, late = (last - first for first, last in cuts(per))
+    places[...] = jnp.where(
+        slot < early, owner * early + slot, owners * early + owner * late + slot - early
+    )
 
 
 def reach(adjacent_three, valid_three, labelled, adjacent_two, valid_two, rows_all, per):
     targets, fan = adjacent_two.shape
+    seeds = labelled.shape[0]
     deep = up(up(rows_all, SPAN) // LANES, 16)
     area = max(fan * targets, rows_all)
     return call(
@@ -210,10 +229,12 @@
         (
             jax.ShapeDtypeStruct((deep, LANES), jnp.int32),
             jax.ShapeDtypeStruct((deep, LANES), jnp.int32),
+            jax.ShapeDtypeStruct((targets, 16), jnp.int32),
+            jax.ShapeDtypeStruct((seeds, 8), jnp.int32),
             jax.ShapeDtypeStruct((2,), jnp.int32),
         ),
-        [vmem] * 7,
-        (vmem, vmem, smem),
+        [vmem] * 5,
+        (vmem,) * 4 + (smem,),
         [
             pltpu.VMEM((2 * deep, area), jnp.bfloat16),
             pltpu.VMEM((area, LANES), jnp.bfloat16),
@@ -221,41 +242,51 @@
         1 << 28,
         1 << 20,
         8 << 20,
-    )(
-        adjacent_three,
-        valid_three,
-        labelled,
-        adjacent_two,
-        valid_two,
-        adjacent_two.T,
-        valid_two.T,
-    )
-
-
-def tally_kernel(count, names, slots, *refs):
-    outs = refs[:PARTS]
-    rows, spread, code, buffer, sems = refs[PARTS:]
+    )(adjacent_three.T, valid_three.T, labelled, adjacent_two.T, valid_two.T)
+
+
+def tally_kernel(
+    count, names, adjacent, valid, early_out, late_out, table, rows, spread, marked, buffer, sems, *, per
+):
     low = jnp.bfloat16
-    wide = outs[0].shape[1]
-    high_all = PARTS * wide // SPAN
-    fan = slots.shape[1]
-    groups = SPAN // fan
+    fan, targets = adjacent.shape
+    unit = spread.shape[0]
+    groups = SPAN // unit
     used = count[1]
-
-    across = lax.broadcasted_iota(jnp.int32, (fan, SPAN), 1)
-    down = lax.broadcasted_iota(jnp.int32, (fan, SPAN), 0)
-    spread[...] = jnp.where(lax.div(across, fan) == down, 1.0, 0.0).astype(low)
-    lane = lax.broadcasted_iota(jnp.int32, (fan, SPAN), 1)
-    place = lax.broadcasted_iota(jnp.int32, (fan, SPAN), 0)
+    outs = (early_out, late_out)
+    first_wide = early_out.shape[1]
+    high_all = (first_wide + late_out.shape[1]) // SPAN
+
+    slot = adjacent[...]
+    owner = lax.shift_right_logical(slot, per.bit_length() - 1)
+    inner = slot & (per - 1)
+    early, late = (last - first for first, last in cuts(per))
+    slot = jnp.where(
+        inner < early, owner * early + inner, first_wide + owner * late + inner - early
+    )
+    slot = jnp.where(valid[...] > 0, slot, -1)
+    slot = jnp.concatenate([slot, jnp.full((unit - fan, targets), -1, jnp.int32)], axis=0)
+    slot = slot.astype(jnp.float32)
+    for b in range(0, targets, LANES):
+        table[b : b + LANES, :] = jnp.transpose(slot[:, b : b + LANES]).astype(jnp.int32)
+    table[targets:, :] = jnp.full((table.shape[0] - targets, unit), -1, jnp.int32)
+
+    across = lax.broadcasted_iota(jnp.int32, (unit, SPAN), 1)
+    down = lax.broadcasted_iota(jnp.int32, (unit, SPAN), 0)
+    spread[...] = jnp.where(lax.div(across, unit) == down, 1.0, 0.0).astype(low)
+    lane = across.astype(jnp.float32).astype(low)
+    one = jnp.ones((unit, SPAN), low)
+    zero = jnp.zeros((unit, SPAN), low)
 
     def copies(block, slot):
+        where = pl.ds(pl.multiple_of(block * SPAN, SPAN), SPAN)
         return [
             pltpu.make_async_copy(
-                buffer.at[slot, :, pl.ds(part * wide, wide)],
-                outs[part].at[pl.ds(pl.multiple_of(block * SPAN, SPAN), SPAN), :],
-                sems.at[slot, part],
+                buffer.at[slot, :, pl.ds(which * first_wide, out.shape[1])],
+                out.at[where, :],
+                sems.at[slot, which],
             )
-            for part in range(PARTS)
+            for which, out in enumerate(outs)
         ]
 
     def body(block, carry):
@@ -266,44 +297,43 @@
             for copy in copies(block - 2, slot):
                 copy.wait()
 
-        copy_rows(names, block, slots, rows)
-        row = rows[...]
-        high = lax.shift_right_arithmetic(row, 8).astype(jnp.float32).astype(low)
-        lined = dot(high, spread[...])
-        own = lax.rem(lax.broadcasted_iota(jnp.int32, (SPAN, SPAN), 0), fan) == lax.rem(
-            lax.broadcasted_iota(jnp.int32, (SPAN, SPAN), 1), fan
+        copy_rows(names, block, table, rows)
+        high = lax.shift_right_arithmetic(rows[...], 8).astype(jnp.float32).astype(low)
+        own = lax.rem(lax.broadcasted_iota(jnp.int32, (SPAN, SPAN), 0), unit) == lax.rem(
+            lax.broadcasted_iota(jnp.int32, (SPAN, SPAN), 1), unit
         )
-        lined = jnp.where(own, lined, 0.0).astype(low)
-        member = (
-            lax.div(lax.broadcasted_iota(jnp.int32, (groups, SPAN), 1), fan)
-            == lax.broadcasted_iota(jnp.int32, (groups, SPAN), 0)
-        )
-        gathered = dot(jnp.where(member, 1.0, 0.0).astype(low), lined).astype(jnp.int32)
-        code[...] = gathered * fan + lax.rem(
-            lax.broadcasted_iota(jnp.int32, (groups, SPAN), 1), fan
-        )
-
-        def group(g, inner):
-            first = pl.multiple_of(g * fan, fan)
-            rest = rows[pl.ds(first, fan), :] & (SPAN - 1)
+        marked[...] = jnp.where(own, dot(high, spread[...]), -1.0).astype(low)
+
+        def single(g):
+            first = pl.multiple_of(g * unit, unit)
+            rest = (rows[pl.ds(first, unit), :] & (SPAN - 1)).astype(jnp.float32)
             columns = [
-                jnp.where(jnp.broadcast_to(rest[:, j : j + 1], (fan, SPAN)) == lane, 1.0, 0.0)
-                for j in range(fan)
+                jnp.where(
+                    jnp.broadcast_to(rest[:, j : j + 1], (unit, SPAN)).astype(low) == lane,
+                    one,
+                    zero,
+                )
+                for j in range(unit)
             ]
-            columns = jnp.concatenate(columns, axis=0).astype(low)
-            line = jnp.broadcast_to(code[pl.ds(g, 1), :], (fan, SPAN))
+            mark = marked[pl.ds(first, unit), :]
             marks = [
-                jnp.where(line == place + q * fan, 1.0, 0.0) for q in range(high_all)
+                jnp.where(mark == jnp.full((unit, SPAN), float(q), low), one, zero)
+                for q in range(high_all)
             ]
-            marks = jnp.concatenate(marks, axis=0).astype(low)
-            result = dot(marks, columns).astype(low)
+            result = dot(
+                jnp.concatenate(marks, axis=0), jnp.concatenate(columns, axis=0)
+            ).astype(low)
             for q in range(high_all):
-                buffer[slot, pl.ds(first, fan), q * SPAN : (q + 1) * SPAN] = result[
-                    q * fan : (q + 1) * fan
+                buffer[slot, pl.ds(first, unit), q * SPAN : (q + 1) * SPAN] = result[
+                    q * unit : (q + 1) * unit
                 ]
+
+        def group(step, inner):
+            for u in range(4):
+                single(step * 4 + u)
             return inner
 
-        lax.fori_loop(0, groups, group, 0)
+        lax.fori_loop(0, groups // 4, group, 0)
         for copy in copies(block, slot):
             copy.start()
         return carry
@@ -321,26 +351,28 @@
             copy.wait()
 
 
-def tally(count, names, slots, padded, total):
-    fan = slots.shape[1]
-    wide = total // PARTS
+def tally(count, names, adjacent, valid, padded, devices, per):
+    targets = adjacent.shape[0]
+    unit = 16
+    wide = [devices * (last - first) for first, last in cuts(per)]
     return call(
-        tally_kernel,
+        functools.partial(tally_kernel, per=per),
         "tally",
-        (jax.ShapeDtypeStruct((padded, wide), jnp.bfloat16),) * PARTS,
-        [smem, smem, vmem],
-        (anywhere,) * PARTS,
+        tuple(jax.ShapeDtypeStruct((padded, item), jnp.bfloat16) for item in wide),
+        [smem, smem, vmem, vmem],
+        (anywhere, anywhere),
         [
-            pltpu.VMEM((SPAN, fan), jnp.int32),
-            pltpu.VMEM((fan, SPAN), jnp.bfloat16),
-            pltpu.VMEM((SPAN // fan, SPAN), jnp.int32),
-            pltpu.VMEM((2, SPAN, total), jnp.bfloat16),
-            pltpu.SemaphoreType.DMA((2, PARTS)),
+            pltpu.VMEM((targets + 8, unit), jnp.int32),
+            pltpu.VMEM((SPAN, unit), jnp.int32),
+            pltpu.VMEM((unit, SPAN), jnp.bfloat16),
+            pltpu.VMEM((SPAN, SPAN), jnp.bfloat16),
+            pltpu.VMEM((2, SPAN, sum(wide)), jnp.bfloat16),
+            pltpu.SemaphoreType.DMA((2, 2)),
         ],
         1 << 32,
         32 << 20,
-        20 << 20,
-    )(count, names, slots)
+        24 << 20,
+    )(count, names, adjacent.T, valid.T)
 
 
 def early_kernel(count, tallies, source, out, table, buffer, result, sems, out_sems):
@@ -411,16 +443,14 @@
     )(count, tallies, source)
 
 
-def link_kernel(count, names, adjacent, valid, out):
-    targets, fan = adjacent.shape
+def link_kernel(count, names, near, out, *, fan):
+    targets = near.shape[0]
     tile = 32
     blocks = count[1]
 
     def rows(step, carry):
         first = pl.multiple_of(step * tile, tile)
-        here = jnp.where(
-            valid[pl.ds(first, tile), :] > 0, adjacent[pl.ds(first, tile), :], -1
-        )
+        here = near[pl.ds(first, tile), :]
         spread = [jnp.broadcast_to(here[:, j : j + 1], (tile, LANES)) for j in range(fan)]
         own = first + lax.broadcasted_iota(jnp.int32, (tile, LANES), 0)
 
@@ -444,20 +474,20 @@
     lax.fori_loop(0, targets // tile, rows, 0)
 
 
-def link_matrix(count, names, adjacent, valid, padded):
+def link_matrix(count, names, near, fan, padded):
     blocks = padded // SPAN
-    targets = adjacent.shape[0]
+    targets = near.shape[0]
     return call(
-        link_kernel,
+        functools.partial(link_kernel, fan=fan),
         "link_matrix",
         jax.ShapeDtypeStruct((blocks, 2 * targets, SPAN), jnp.bfloat16),
-        [smem, vmem, vmem, vmem],
+        [smem, vmem, vmem],
         vmem,
         [],
         blocks * targets * SPAN * 30,
         blocks * targets * SPAN * 4,
         12 << 20,
-    )(count, names, adjacent, valid)
+    )(count, names, near)
 
 
 def step_kernel(
@@ -469,12 +499,11 @@
     links,
     *refs,
     classes,
-    part,
 ):
     sources = refs[:PARTS]
     step_body(
         info, count, places, partial, tallies, links, sources, *refs[PARTS:],
-        classes=classes, part=part,
+        classes=classes,
     )
 
 
@@ -486,9 +515,8 @@
     tallies,
     links,
     sources,
-    valid_two,
-    adjacent_three,
-    valid_three,
+    near_two,
+    near_three,
     labels,
     labelled,
     weights_in,
@@ -515,7 +543,6 @@
     link_sems,
     *,
     classes,
-    part,
 ):
     blocks, both, _ = links.shape
     targets = both // 2
@@ -556,11 +583,11 @@
     lax.fori_loop(0, used, start_link, 0)
     late_table[:, 0:width] = sources[-1][...]
     late_table[:, width:] = jnp.ones((late_table.shape[0], width), low)
-    held = own_table.shape[0] // PARTS
-    for which in range(PARTS):
-        own_table[which * held : (which + 1) * held, :] = sources[which][0:held, :].astype(
-            jnp.float32
-        )
+    filled = 0
+    for source in sources:
+        held = own_table.shape[0] * source.shape[0] // sum(item.shape[0] for item in sources)
+        own_table[filled : filled + held, :] = source[0:held, :].astype(jnp.float32)
+        filled += held
 
     w_in = weights_in[...].astype(low).reshape(2 * weights_in.shape[1], hidden)
     bias_in = biases[:, 0:hidden]
@@ -601,7 +628,7 @@
 
     lax.fori_loop(0, used, forward, 0)
     total = sums[...]
-    counts_two = clipped_counts(valid_two[...])
+    counts_two = clipped_counts(near_two[...] >= 0)
     mixed_one = (total[0:targets] / counts_two).astype(low)
     self_one = total[targets:].astype(low)
     w_mid = weights_mid[...].astype(low)
@@ -611,13 +638,13 @@
     slope_mid = s * (1.0 + z * (1.0 - s))
     hidden_two = (z * s).astype(low)
 
-    here = jnp.where(valid_three[...] > 0, adjacent_three[...], -1)
+    here = near_three[...]
     place = lax.broadcasted_iota(jnp.int32, (seeds, targets), 1)
     number = jnp.zeros((seeds, targets), jnp.float32)
     for j in range(here.shape[1]):
         number = number + jnp.where(here[:, j : j + 1] == place, 1.0, 0.0)
     number = number.astype(low)
-    counts_three = clipped_counts(valid_three[...])
+    counts_three = clipped_counts(here >= 0)
     mixed_two = (dot(number, hidden_two) / counts_three).astype(low)
     self_two = hidden_two[0:seeds]
     w_out = [
@@ -688,17 +715,17 @@
     send[...] = packed[pl.ds(pl.multiple_of((1 - core) * half, 16), half), :].astype(low)
 
 
-def run_step(info, count, places, partial, tallies, links, sources, rest, half, classes, part, owners):
+def run_step(info, count, places, partial, tallies, links, sources, rest, half, classes, held):
     padded = partial.shape[0]
     blocks, both, _ = links.shape
-    total, width = sources[0].shape
-    hidden = rest[5].shape[2]
+    total, width = sources[-1].shape
+    hidden = rest[4].shape[2]
     wide = up(classes, LANES)
     return call(
-        functools.partial(step_kernel, classes=classes, part=part),
+        functools.partial(step_kernel, classes=classes),
         "step",
         (jax.ShapeDtypeStruct((half, LANES), jnp.bfloat16),) * 2,
-        [smem] * 3 + [anywhere] * 3 + [vmem] * (PARTS + 9),
+        [smem] * 3 + [anywhere] * 3 + [vmem] * (PARTS + 8),
         (vmem, vmem),
         [
             pltpu.VMEM((padded, hidden), jnp.float32),
@@ -707,7 +734,7 @@
             pltpu.VMEM((2 * width, hidden), jnp.float32),
             pltpu.VMEM((2 * hidden, hidden), jnp.float32),
             pltpu.VMEM((wide, 2 * hidden), jnp.float32),
-            pltpu.VMEM((PARTS * owners * part, width), jnp.float32),
+            pltpu.VMEM((held, width), jnp.float32),
             pltpu.VMEM((total, 2 * width), jnp.bfloat16),
             pltpu.VMEM((padded, 2 * width), jnp.bfloat16),
             pltpu.VMEM((SPAN, width), jnp.float32),
@@ -719,8 +746,8 @@
             pltpu.SemaphoreType.DMA((blocks,)),
         ],
         4 << 30,
-        32 << 20,
-        44 << 20,
+        16 << 20,
+        36 << 20,
     )(info, count, places, partial, tallies, links, *sources, *rest)
 
 
@@ -896,7 +923,7 @@
         [pltpu.VMEM((2 * mine.shape[0], LANES), jnp.bfloat16)],
         1 << 30,
         10 << 20,
-        32 << 20,
+        16 << 20,
     )(info, fixes, corners, mine, theirs, *vectors, *flat)
 
 
@@ -935,53 +962,64 @@
 ):
     width = features.shape[1]
     devices, per = requests.shape
-    part = per // PARTS
-    total = devices * per
-    targets, fan = adjacent_one.shape
+    targets = adjacent_one.shape[0]
     padded = up(targets, SPAN)
-    owners = -(-targets // per)
     classes = weights_out.shape[2]
     hidden = weights_in.shape[2]
     core = lax.axis_index("core")
     own = lax.axis_index(PEERS)
 
     wanted = lax.all_to_all(requests, AXES, split_axis=0, concat_axis=0, tiled=True)
-    sources = []
-    for which in range(PARTS):
-        found = pick_rows(wanted, features, which).reshape(devices, part, width)
-        pulled = lax.all_to_all(found, AXES, split_axis=0, concat_axis=0, tiled=True)
-        sources.append(pulled.reshape(devices * part, width))
-
-    names, places, count = reach(
+    names, places, near_two, near_three, count = reach(
         adjacent_three, valid_three, labelled, adjacent_two, valid_two, targets, per
     )
-    owner, slot = adjacent_one // per, adjacent_one % per
-    slots = (slot // part) * (devices * part) + owner * part + slot % part
-    slots = jnp.where(valid_one > 0, slots, -1)
-    slots = jnp.pad(slots, ((0, 8), (0, 16 - fan)), constant_values=-1)
-    tallies = tally(count, names, slots, padded, total)
-    links = link_matrix(count, names, adjacent_two, valid_two, padded)
-    partial = early_sums(count, tallies[0], sources[0])
+    wanted, count = lax.optimization_barrier((wanted.reshape(-1), count))
+    early_cut, late_cut = cuts(per)
+
+    def trade(found):
+        pulled = lax.all_to_all(
+            found.reshape(devices, -1, width), AXES, split_axis=0, concat_axis=0, tiled=True
+        )
+        return pulled.reshape(-1, width)
+
+    early_source = trade(pick_rows(wanted, features, per, early_cut))
+    found = pick_rows(wanted, features, per, late_cut)
+    links = link_matrix(count, names, near_two, adjacent_two.shape[1], padded)
+    names, places = names.reshape(-1), places.reshape(-1)
+    early_tally, late_tally = tally(count, names, adjacent_one, valid_one, padded, devices, per)
+
+    core_info = jnp.stack([core, ((core == 1) & (own == peers - 1)).astype(jnp.int32)])
+    core_info = core_info.astype(jnp.int32)
+    stepped = step_count.astype(jnp.float32)
+    fixes = jnp.stack([1.0 - 0.9**stepped, 1.0 - 0.95**stepped])
+    corners = jnp.concatenate(
+        [
+            item[:, 0, 0]
+            for item in (left_in, right_in, left_mid, right_mid, right_out, left_out)
+        ]
+    )
+    found, early_tally, info, fixes, corners = lax.optimization_barrier(
+        (found, early_tally, core_info, fixes, corners)
+    )
+    late_source = trade(found)
+    partial = early_sums(count, early_tally, early_source)
 
     rows = (2 * width + 2 * weights_mid.shape[1]) * (hidden // LANES)
     rows += up(classes, 16) * (2 * hidden // LANES)
     each = up(-(-(rows + 16) // (2 * peers)), 8)
     half = each * peers
-    info = jnp.stack([core, ((core == 1) & (own == peers - 1)).astype(jnp.int32)])
-    info = info.astype(jnp.int32)
     turned_out = weights_out.transpose(2, 0, 1)
     keep, send = run_step(
         info,
         count,
         places,
         partial,
-        tallies[1],
+        late_tally,
         links,
-        sources,
+        (early_source, late_source),
         (
-            valid_two,
-            adjacent_three,
-            valid_three,
+            near_two,
+            near_three,
             labels,
             labelled,
             weights_in,
@@ -991,8 +1029,7 @@
         ),
         half,
         classes,
-        part,
-        owners,
+        -(-targets // per) * per,
     )
     swap = [(0, 1), (1, 0)]
     theirs = lax.ppermute(send, "core", swap)
@@ -1003,14 +1040,6 @@
     mine = mine.reshape(half, LANES)
     theirs = lax.ppermute(mine, "core", swap)
 
-    stepped = step_count.astype(jnp.float32)
-    fixes = jnp.stack([1.0 - 0.9**stepped, 1.0 - 0.95**stepped])
-    corners = jnp.concatenate(
-        [
-            item[:, 0, 0]
-            for item in (left_in, right_in, left_mid, right_mid, right_out, left_out)
-        ]
-    )
     outs = run_update(
         info,
         fixes,

time: 211 us -> 168 us (0.80)
  blocking collectives: 85.2 us -> 50.8 us
  Pallas kernels: 56.7 us -> 37.3 us
  waiting for transfers between devices: 16.4 us -> 24.5 us
  local copies, waits for them, and re-layouts: 24.1 us -> 31 us
  other arithmetic: 5.57 us -> 0.15 us
    all_to_all x1, blocking collectives: 70.9 us -> 37.5 us  [body(): lax.all_to_all(summed, PEERS, split_axis=0, concat_axis=0, tiled=True)]
    pallas_call x5, Pallas kernels: 44.8 us -> 25.7 us  [the longest x2 11.1 us: pick_rows(): call(functools.partial(pick_kernel, first=first, last=last, per=per), 'pi...]
    all_to_all x3, starting transfers between devices: 8.98 us -> 19.6 us  [the longest x2 12.3 us: trade(): lax.all_to_all(found.reshape(devices, -1, width), AXES, split_axis=0, con...]
    ppermute x1, starting transfers between devices: 10.9 us -> 1.63 us  [body(): theirs = lax.ppermute(send, 'core', swap)]
    unnamed x56, local copies, waits for them, and re-layouts: 18.9 us -> 26.3 us
    all_to_all x3, waiting for transfers between devices: 15.1 us -> 21.7 us  [the longest x2 20.7 us: trade(): lax.all_to_all(found.reshape(devices, -1, width), AXES, split_axis=0, con...]
    select_n x1 -> x0, other arithmetic: 5.38 us -> none  [body(): slots = jnp.where(valid_one > 0, slots, -1)]
  transfers between devices with their start and end apart: 5 -> 5, of which waited for: 3 -> 5; matrix products, arithmetic and copies ran while one was open for 6% -> 2% of each run, Pallas kernels for 14% -> 11%
where the time goes in v3:
time: 168 us; the launch traced here: 167 us
  blocking collectives  50.8 us (30%)
  Pallas kernels  37.3 us (22%)
  local copies, waits for them, and re-layouts  31 us (18%)
  waiting for transfers between devices  24.5 us (15%)
  starting transfers between devices  21.2 us (13%)
  between operations  1.81 us (1%)
    all_to_all x1, blocking collectives, body(): lax.all_to_all(summed, PEERS, split_axis=0, concat_axis=0, tiled=True)  37.5 us
    unnamed x56, local copies, waits for them, and re-layouts  26.3 us
    all_to_all x2, waiting for transfers between devices, trade(): lax.all_to_all(found.reshape(devices, -1, width), AXES, split_axis=0, con...  20.7 us
    all_to_all x1, blocking collectives, body(): lax.all_to_all(shared, PEERS, split_axis=0, concat_axis=0, tiled=True)  13.3 us
    all_to_all x2, starting transfers between devices, trade(): lax.all_to_all(found.reshape(devices, -1, width), AXES, split_axis=0, con...  12.3 us
    pallas_call x2, Pallas kernels, pick_rows(): call(functools.partial(pick_kernel, first=first, last=last, per=per), 'pi...  11.1 us
    all_to_all x1, starting transfers between devices, body(): lax.all_to_all(requests, AXES, split_axis=0, concat_axis=0, tiled=True)  7.3 us
    pallas_call x1, Pallas kernels, run_step(): call(functools.partial(step_kernel, classes=classes), 'step', (jax.ShapeD...  6.04 us
  transfers between devices with their start and end apart: 5, of which 5 were waited for; matrix products, arithmetic and copies ran while one was open for 2% of the time, Pallas kernels for 11%

profile of v3, /device:TPU:0, one launch (start us, length us, event | category | flops | bytes accessed | tf_op | source)
XLA Modules:
  0.0 166.8 jit_solution(16114660467911316649)
XLA Ops:
  0.6 1.4 all_to_all.18
  2.0 7.3 %all-to-all-start = ((s32[32,1,256]{2,1,0:T(1,128)}), s32[32,1,256]{2,1,0:T(1,128)S(1)}, u32[]{:S(2)}, u32[]{:S(2)}) async-start(s32[32,1,256]{2,1,0:T(1,128)} %all_to_all.18), calls=%async_computation | async-start | bytes 65536 | tf_op jit(solution)/shard_map/all_to_all | solution.py:972
  9.3 0.0 copy-start.19
  9.4 0.6 copy-done.19
  10.0 0.7 copy-done.24
  10.7 0.7 copy-done.25
  11.5 0.7 copy-done.26
  12.2 0.7 copy-done.27
  12.9 2.6 %reach.1 = (s32[48,128]{1,0:T(8,128)S(1)}, s32[48,128]{1,0:T(8,128)S(1)}, s32[384,16]{1,0:T(8,128)S(1)}, s32[64,8]{1,0:T(8,128)S(1)}, s32[2]{0:T(128)S(1)}) custom-call(s32[5,64]{1,0:T(8,128)S(1)} %bitcast.42, s32[5,64]{1,0:T(8,128)S(1)} %bitcast.43, s32[64]{0:T(128)S(1)} %copy-done.19, s32[10,384]{1,0:T(8,128)S(1)} %bitcast.40, s32[10,384]{1,0:T(8,128)S(1)} %bitcast.41), custom_call_target="tpu_custom_call" | custom-call | flops 268435456 | bytes 1048576 | tf_op jit(solution)/shard_map/reach/pallas_call | solution.py:226
  15.5 1.0 all-to-all-done
  16.5 3.4 %copy-done = f32[16384,128]{1,0:T(8,128)S(1)} copy-done((f32[16384,128]{1,0:T(8,128)S(1)}, f32[16384,128]{1,0:T(8,128)}, u32[]{:S(2)}) %copy-start) | copy-done | bytes 8388632
  19.9 7.4 %pick_rows.3 = bf16[6144,128]{1,0:T(8,128)(2,1)} custom-call(s32[8192]{0:T(1024)S(1)} %bitcast.34, f32[16384,128]{1,0:T(8,128)S(1)} %copy-done), custom_call_target="tpu_custom_call" | custom-call | flops 786432 | bytes 8388608 | tf_op jit(solution)/shard_map/pick_rows/pallas_call | solution.py:107
  27.3 4.8 %all-to-all-start.1 = ((bf16[32,192,128]{2,1,0:T(8,128)(2,1)}), bf16[32,192,128]{2,1,0:T(8,128)(2,1)S(1)}, u32[]{:S(2)}, u32[]{:S(2)}) async-start(bf16[32,192,128]{2,1,0:T(8,128)(2,1)} %bitcast.13), calls=%async_computation.1 | async-start | bytes 3145728 | tf_op jit(solution)/shard_map/all_to_all | solution.py:980
  32.9 0.8 slice_reduce_fusion.1
  33.7 0.8 slice_reduce_fusion.5
  34.5 0.8 slice_reduce_fusion
  35.3 0.8 slice_reduce_fusion.3
  36.1 0.1 concatenate.3.corners
  36.2 0.1 pad_add_fusion.info
  36.3 0.1 pad_maximum_fusion.fixes
  36.4 3.4 %copy-done.1 = f32[16384,128]{1,0:T(8,128)S(1)} copy-done((f32[16384,128]{1,0:T(8,128)S(1)}, f32[16384,128]{1,0:T(8,128)}, u32[]{:S(2)}) %copy-start.1) | copy-done | bytes 8388632
  39.7 3.7 %pick_rows.2 = bf16[2048,128]{1,0:T(8,128)(2,1)} custom-call(s32[8192]{0:T(1024)S(1)} %bitcast.35, f32[16384,128]{1,0:T(8,128)S(1)} %copy-done.1), custom_call_target="tpu_custom_call" | custom-call | flops 262144 | bytes 8388608 | tf_op jit(solution)/shard_map/pick_rows/pallas_call | solution.py:107
  43.4 6.0 %tally.1 = (bf16[4352,6144]{1,0:T(8,128)(2,1)}, bf16[4352,2048]{1,0:T(8,128)(2,1)S(1)}) custom-call(s32[2]{0:T(128)S(1)} %get-tuple-element.50.count, s32[6144]{0:T(1024)S(1)} %bitcast.37, s32[15,4224]{1,0:T(8,128)S(1)} %bitcast.38, s32[15,4224]{1,0:T(8,128)S(1)} %bitcast.39), custom_call_target="tpu_custom_call" | custom-call | flops 4294967296 | bytes 33554432 | tf_op jit(solution)/shard_map/tally/pallas_call | solution.py:358
  49.5 6.0 %copy-done.6 = bf16[4352,2048]{1,0:T(8,128)(2,1)} copy-done((bf16[4352,2048]{1,0:T(8,128)(2,1)}, bf16[4352,2048]{1,0:T(8,128)(2,1)S(1)}, u32[]{:S(2)}) %copy-start.6) | copy-done | bytes 17825816
  55.5 15.5 %all-to-all-done.1 = bf16[32,192,128]{2,1,0:T(8,128)(2,1)S(1)} async-done(((bf16[32,192,128]{2,1,0:T(8,128)(2,1)}), bf16[32,192,128]{2,1,0:T(8,128)(2,1)S(1)}, u32[]{:S(2)}, u32[]{:S(2)}) %all-to-all-start.1) | async-done | bytes 1572896 | tf_op jit(solution)/shard_map/all_to_all | solution.py:980
  71.0 7.4 %all-to-all-start.2 = ((bf16[32,64,128]{2,1,0:T(8,128)(2,1)}), bf16[32,64,128]{2,1,0:T(8,128)(2,1)S(1)}, u32[]{:S(2)}, u32[]{:S(2)}) async-start(bf16[32,64,128]{2,1,0:T(8,128)(2,1)} %bitcast.15), calls=%async_computation.2 | async-start | bytes 1048576 | tf_op jit(solution)/shard_map/all_to_all | solution.py:980
  78.4 2.5 %link_matrix.1.links = bf16[17,768,256]{2,1,0:T(8,128)(2,1)S(1)} custom-call(s32[2]{0:T(128)S(1)} %get-tuple-element.50.count, s32[48,128]{1,0:T(8,128)S(1)} %get-tuple-element.51.names, s32[384,16]{1,0:T(8,128)S(1)} %get-tuple-element.59.near.refs_2_), custom_call_target="tpu_custom_call" | custom-call | flops 50135040 | bytes 6684672 | tf_op jit(solution)/shard_map/link_matrix/pallas_call | solution.py:480
  81.0 2.7 %copy-done.2 = bf16[17,768,256]{2,1,0:T(8,128)(2,1)} copy-done((bf16[17,768,256]{2,1,0:T(8,128)(2,1)}, bf16[17,768,256]{2,1,0:T(8,128)(2,1)S(1)}, u32[]{:S(2)}) %copy-start.2) | copy-done | bytes 6684696
  83.7 0.0 copy-start.20
  83.7 0.0 copy-start.21
  83.7 3.7 %early_sums.1.partial = f32[4352,256]{1,0:T(8,128)S(1)} custom-call(s32[2]{0:T(128)S(1)} %get-tuple-element.50.count, bf16[4352,6144]{1,0:T(8,128)(2,1)} %get-tuple-element.57.tallies, bf16[6144,128]{1,0:T(8,128)(2,1)S(1)} %bitcast.25), custom_call_target="tpu_custom_call" | custom-call | flops 4294967296 | bytes 16777216 | tf_op jit(solution)/shard_map/early_sums/pallas_call | solution.py:427
  87.5 2.0 %copy-done.4 = f32[4352,256]{1,0:T(8,128)} copy-done((f32[4352,256]{1,0:T(8,128)}, f32[4352,256]{1,0:T(8,128)S(1)}, u32[]{:S(2)}) %copy-start.4) | copy-done | bytes 4456472
  89.5 5.2 %all-to-all-done.2 = bf16[32,64,128]{2,1,0:T(8,128)(2,1)S(1)} async-done(((bf16[32,64,128]{2,1,0:T(8,128)(2,1)}), bf16[32,64,128]{2,1,0:T(8,128)(2,1)S(1)}, u32[]{:S(2)}, u32[]{:S(2)}) %all-to-all-start.2) | async-done | bytes 524320 | tf_op jit(solution)/shard_map/all_to_all | solution.py:980
  94.8 2.9 %copy-done.3 = bf16[17,768,256]{2,1,0:T(8,128)(2,1)S(1)} copy-done((bf16[17,768,256]{2,1,0:T(8,128)(2,1)S(1)}, bf16[17,768,256]{2,1,0:T(8,128)(2,1)}, u32[]{:S(2)}) %copy-start.3) | copy-done | bytes 6684696
  97.7 2.3 %copy-done.5 = f32[4352,256]{1,0:T(8,128)S(1)} copy-done((f32[4352,256]{1,0:T(8,128)S(1)}, f32[4352,256]{1,0:T(8,128)}, u32[]{:S(2)}) %copy-start.5) | copy-done | bytes 4456472
  100.0 0.0 copy-start.14
  100.0 0.0 copy-start.15
  100.0 0.0 copy-start.17
  100.0 0.0 copy-start.18
  100.0 6.0 %step.1 = (bf16[1152,128]{1,0:T(8,128)(2,1)S(1)}, bf16[1152,128]{1,0:T(8,128)(2,1)S(1)}) custom-call(s32[2]{0:T(128)S(1)} %pad_add_fusion.info, s32[2]{0:T(128)S(1)} %get-tuple-element.50.count, s32[6144]{0:T(1024)S(1)} %bitcast.36, f32[4352,256]{1,0:T(8,128)S(1)} %copy-done.5, bf16[4352,2048]{1,0:T(8,128)(2,1)} %copy-done.6, ...), custom_call_target="tpu_custom_call" | custom-call | flops 4294967296 | bytes 16777216 | tf_op jit(solution)/shard_map/step/pallas_call | solution.py:724
  106.1 1.6 collective-permute-start
  107.7 1.2 collective-permute-done.theirs
  108.9 0.6 pair_sum.1
  109.6 37.5 %all_to_all.29.pieces = bf16[16,72,128]{2,1,0:T(8,128)(2,1)S(1)} all-to-all(bf16[16,72,128]{2,1,0:T(8,128)(2,1)S(1)} %bitcast.32), channel_id=1, replica_groups=mesh['chip'=2,'core'=2,'dev'=8] {'chip','dev'}, dimensions={0} | all-to-all | bytes 589824 | tf_op jit(solution)/shard_map/all_to_all | solution.py:1037
  147.0 0.6 spread_sum.1
  147.6 13.3 %all_to_all.30 = bf16[16,72,128]{2,1,0:T(8,128)(2,1)S(1)} all-to-all(bf16[16,72,128]{2,1,0:T(8,128)(2,1)S(1)} %spread_sum.1), channel_id=1, replica_groups=mesh['chip'=2,'core'=2,'dev'=8] {'chip','dev'}, dimensions={0} | all-to-all | bytes 589824 | tf_op jit(solution)/shard_map/all_to_all | solution.py:1039
  160.9 1.6 collective-permute-done.1.theirs
  162.6 4.0 %update.1 = (f32[1,1]{1,0:T(1,128)}, f32[2,128,256]{2,1,0:T(8,128)}, bf16[2,128,256]{2,1,0:T(8,128)(2,1)}, f32[2,128,128]{2,1,0:T(8,128)}, f32[2,256,256]{2,1,0:...) custom-call(s32[2]{0:T(128)S(1)} %pad_add_fusion.info, ...), custom_call_target="tpu_custom_call" | custom-call | flops 1073741824 | bytes 10485760 | tf_op jit(solution)/shard_map/update/pallas_call | solution.py:917
  (38 shorter events, 0.1 us)
Async XLA Ops:
  2.0 14.5 %all-to-all-start = ((s32[32,1,256]{2,1,0:T(1,128)}), s32[32,1,256]{2,1,0:T(1,128)S(1)}, u32[]{:S(2)}, u32[]{:S(2)}) async-start(s32[32,1,256]{2,1,0:T(1,128)} %all_to_all.18), calls=%async_computation | async-start | bytes 65536 | tf_op jit(solution)/shard_map/all_to_all | solution.py:972
  9.3 0.7 copy-start.19
  10.0 0.7 copy-start.24
  10.7 0.7 copy-start.25
  11.5 0.7 copy-start.26
  12.2 0.7 copy-start.27
  16.5 3.4 %copy-start = (f32[16384,128]{1,0:T(8,128)S(1)}, f32[16384,128]{1,0:T(8,128)}, u32[]{:S(2)}) copy-start(f32[16384,128]{1,0:T(8,128)} %table.3) | copy-start | bytes 25165828
  27.3 16.1 %copy-start.22 = (s32[4224,15]{0,1:T(8,128)S(1)}, s32[4224,15]{0,1:T(8,128)}, u32[]{:S(2)}) copy-start(s32[4224,15]{0,1:T(8,128)} %param.31) | copy-start | bytes 760324
  27.3 16.1 %copy-start.23 = (s32[4224,15]{0,1:T(8,128)S(1)}, s32[4224,15]{0,1:T(8,128)}, u32[]{:S(2)}) copy-start(s32[4224,15]{0,1:T(8,128)} %param.34) | copy-start | bytes 760324
  27.3 43.7 %all-to-all-start.1 = ((bf16[32,192,128]{2,1,0:T(8,128)(2,1)}), bf16[32,192,128]{2,1,0:T(8,128)(2,1)S(1)}, u32[]{:S(2)}, u32[]{:S(2)}) async-start(bf16[32,192,128]{2,1,0:T(8,128)(2,1)} %bitcast.13), calls=%async_computation.1 | async-start | bytes 3145728 | tf_op jit(solution)/shard_map/all_to_all | solution.py:980
  36.3 3.4 %copy-start.1 = (f32[16384,128]{1,0:T(8,128)S(1)}, f32[16384,128]{1,0:T(8,128)}, u32[]{:S(2)}) copy-start(f32[16384,128]{1,0:T(8,128)} %table.3) | copy-start | bytes 25165828
  49.5 6.0 %copy-start.6 = (bf16[4352,2048]{1,0:T(8,128)(2,1)}, bf16[4352,2048]{1,0:T(8,128)(2,1)S(1)}, u32[]{:S(2)}) copy-start(bf16[4352,2048]{1,0:T(8,128)(2,1)S(1)} %get-tuple-element.58.tallies) | copy-start | bytes 53477380
  71.0 23.8 %all-to-all-start.2 = ((bf16[32,64,128]{2,1,0:T(8,128)(2,1)}), bf16[32,64,128]{2,1,0:T(8,128)(2,1)S(1)}, u32[]{:S(2)}, u32[]{:S(2)}) async-start(bf16[32,64,128]{2,1,0:T(8,128)(2,1)} %bitcast.15), calls=%async_computation.2 | async-start | bytes 1048576 | tf_op jit(solution)/shard_map/all_to_all | solution.py:980
  81.0 2.7 %copy-start.2 = (bf16[17,768,256]{2,1,0:T(8,128)(2,1)}, bf16[17,768,256]{2,1,0:T(8,128)(2,1)S(1)}, u32[]{:S(2)}) copy-start(bf16[17,768,256]{2,1,0:T(8,128)(2,1)S(1)} %link_matrix.1.links) | copy-start | bytes 20054020
  83.7 11.1 %copy-start.7 = (f32[2,256,256]{2,1,0:T(8,128)S(1)}, f32[2,256,256]{2,1,0:T(8,128)}, u32[]{:S(2)}) copy-start(f32[2,256,256]{2,1,0:T(8,128)} %refs_3_.1) | copy-start | bytes 1572868
  83.7 11.1 %copy-start.8 = (f32[2,256,172]{1,0,2:T(2,128)S(1)}, f32[2,256,172]{1,0,2:T(2,128)}, u32[]{:S(2)}) copy-start(f32[2,256,172]{1,0,2:T(2,128)} %param.41) | copy-start | bytes 1056772
  83.7 11.1 %copy-start.9 = (f32[2,128,256]{2,1,0:T(8,128)S(1)}, f32[2,128,256]{2,1,0:T(8,128)}, u32[]{:S(2)}) copy-start(f32[2,128,256]{2,1,0:T(8,128)} %refs_0_.1) | copy-start | bytes 786436
  83.7 11.1 %copy-start.16 = (f32[684]{0:T(1024)S(1)}, f32[684]{0:T(1024)}, u32[]{:S(2)}) copy-start(f32[684]{0:T(1024)} %biases.1) | copy-start | bytes 8212
  83.7 11.1 %copy-start.20 = (s32[64]{0:T(128)S(1)}, s32[64]{0:T(128)}, u32[]{:S(2)}) copy-start(s32[64]{0:T(128)} %refs_5_.2) | copy-start | bytes 772
  83.7 11.1 %copy-start.21 = (s32[64]{0:T(128)S(1)}, s32[64]{0:T(128)}, u32[]{:S(2)}) copy-start(s32[64]{0:T(128)} %refs_4_.2) | copy-start | bytes 772
  87.5 2.1 %copy-start.4 = (f32[4352,256]{1,0:T(8,128)}, f32[4352,256]{1,0:T(8,128)S(1)}, u32[]{:S(2)}) copy-start(f32[4352,256]{1,0:T(8,128)S(1)} %early_sums.1.partial) | copy-start | bytes 13369348
  94.8 2.9 %copy-start.3 = (bf16[17,768,256]{2,1,0:T(8,128)(2,1)S(1)}, bf16[17,768,256]{2,1,0:T(8,128)(2,1)}, u32[]{:S(2)}) copy-start(bf16[17,768,256]{2,1,0:T(8,128)(2,1)} %copy-done.2) | copy-start | bytes 20054020
  97.7 2.3 %copy-start.5 = (f32[4352,256]{1,0:T(8,128)S(1)}, f32[4352,256]{1,0:T(8,128)}, u32[]{:S(2)}) copy-start(f32[4352,256]{1,0:T(8,128)} %copy-done.4) | copy-start | bytes 13369348
  100.0 62.5 %copy-start.10 = (f32[2,256,256]{2,1,0:T(8,128)S(1)}, f32[2,256,256]{2,1,0:T(8,128)}, u32[]{:S(2)}) copy-start(f32[2,256,256]{2,1,0:T(8,128)} %refs_2_.1) | copy-start | bytes 1572868
  100.0 62.5 %copy-start.11 = (f32[2,256,256]{2,1,0:T(8,128)S(1)}, f32[2,256,256]{2,1,0:T(8,128)}, u32[]{:S(2)}) copy-start(f32[2,256,256]{2,1,0:T(8,128)} %refs_4_.3) | copy-start | bytes 1572868
  100.0 62.5 %copy-start.12 = (f32[2,256,256]{2,1,0:T(8,128)S(1)}, f32[2,256,256]{2,1,0:T(8,128)}, u32[]{:S(2)}) copy-start(f32[2,256,256]{2,1,0:T(8,128)} %refs_5_.3) | copy-start | bytes 1572868
  100.0 62.5 %copy-start.13 = (f32[2,256,256]{2,1,0:T(8,128)S(1)}, f32[2,256,256]{2,1,0:T(8,128)}, u32[]{:S(2)}) copy-start(f32[2,256,256]{2,1,0:T(8,128)} %refs_8_.1) | copy-start | bytes 1572868
  100.0 62.5 %copy-start.14 = (f32[2,172,172]{2,0,1:T(2,128)S(1)}, f32[2,172,172]{2,0,1:T(2,128)}, u32[]{:S(2)}) copy-start(f32[2,172,172]{2,0,1:T(2,128)} %param.57) | copy-start | bytes 710020
  100.0 62.5 %copy-start.15 = (f32[2,128,128]{2,1,0:T(8,128)S(1)}, f32[2,128,128]{2,1,0:T(8,128)}, u32[]{:S(2)}) copy-start(f32[2,128,128]{2,1,0:T(8,128)} %refs_1_.1) | copy-start | bytes 393220
  100.0 62.5 %copy-start.17 = (f32[684]{0:T(1024)S(1)}, f32[684]{0:T(1024)}, u32[]{:S(2)}) copy-start(f32[684]{0:T(1024)} %moment_one.1) | copy-start | bytes 8212
  100.0 62.5 %copy-start.18 = (f32[684]{0:T(1024)S(1)}, f32[684]{0:T(1024)}, u32[]{:S(2)}) copy-start(f32[684]{0:T(1024)} %moment_two.1) | copy-start | bytes 8212
  106.1 2.8 %collective-permute-start = (bf16[1152,128]{1,0:T(8,128)(2,1)S(1)}, bf16[1152,128]{1,0:T(8,128)(2,1)S(1)}, u32[]{:S(2)}, u32[]{:S(2)}) collective-permute-start(bf16[1152,128]{1,0:T(8,128)(2,1)S(1)} %get-tuple-element.63), channel_id=1, source_target_pairs={{0,8},{8,0},{1,9},{9,1},{2,10},{10,2},{3,11},{11,3},{4,12},{12,4},... | collective-permute-start | bytes 884744 | tf_op jit(solution)/shard_map/ppermute | solution.py:1035
  160.9 1.6 collective-permute-start.1
